TPU v7x, 128 devices: a whole 4x4x4 slice. The times are simulated.
128 devices in a mesh: site: 4 (over z), blk: 16 (over x, y), charge: 2 (over core).
Axes of the slice: x: 4, y: 4, z: 4, core: 2. Of those that a mesh axis runs over, the one named last changes fastest.
Arguments:
- theta: bfloat16 [4, 64, 128, 2048], P('site', ('blk', 'charge')), may hold values from -6 to 6
- boundary_env: bfloat16 [64, 18, 128, 128], P(('blk', 'charge')), may hold values from -1 to 1
- right_env: bfloat16 [4, 64, 18, 128, 128], P('site', ('blk', 'charge')), may hold values from -1 to 1
- site_tensors: bfloat16 [4, 2, 64, 4, 128, 128], P('site', None, ('blk', 'charge')), may hold values from -0.375 to 0.375
- site_mpo: bfloat16 [4, 2, 18, 18, 4, 4], P('site'), may hold values from -0.75 to 0.75
- bond_ops: bfloat16 [4, 18, 16, 16], P('site'), may hold values from -1 to 1
- block_energy: float32 [4, 64], P('site', ('blk', 'charge')), may hold values from 1 to 4
- sector_charge: int32 [4, 64], P('site', ('blk', 'charge')), may hold values from 0 to 63, as said below
- block_len: int32 [4, 64], P('site', ('blk', 'charge')), may hold values from 64 to 128
- channel_charge: int32 [18], replicated, may hold values from -1 to 1
Outputs:
- env_out: bfloat16 [4, 64, 18, 128, 128], P('site', ('blk', 'charge'))
- lanczos: bfloat16 [4, 64, 128, 2048], P('site', ('blk', 'charge'))
- coefficients: float32 [4, 2], P('site')
Inputs may be any that keep to these rules, and one draw needn't show every extreme that they name: `sector_charge`: in each section every label of 0 to 63 appears exactly once; the blocks held at index c of the charge axis carry labels of parity c.
All inputs are finite; a program needn't handle non-finite values.
Results may differ from a plain program's by a relative error of at most 0.03.
Values may be sent and summed in bfloat16 or wider, within the bound.
A program may use at most 128 MiB of HBM per device.

v0:
```python
import jax
import jax.numpy as jnp
from jax import lax
from jax.sharding import PartitionSpec as P

BS = 128
M = 2048
NS = 64


def from_behind(block, axis, distance):
    devices = range(lax.axis_size(axis))
    route = [(i - distance, i) for i in devices if i - distance in devices]
    return lax.ppermute(block, axis, route)


def from_partner(shard, axis, bit):
    return lax.ppermute(shard, axis, [(i, i ^ 1 << bit) for i in range(lax.axis_size(axis))])


def env_update(environ, tensors, site_op):

    def one_block(entries):
        env_block, site_blocks = entries
        left_part = jnp.einsum(
            "wab,sbc->wsac", env_block, site_blocks, preferred_element_type=jnp.float32
        ).astype(jnp.bfloat16)
        mixed = jnp.einsum(
            "wvts,wsac->vtac", site_op, left_part, preferred_element_type=jnp.float32
        ).astype(jnp.bfloat16)
        return jnp.einsum(
            "tab,vtac->vbc", site_blocks, mixed, preferred_element_type=jnp.float32
        ).astype(jnp.bfloat16)

    return lax.map(one_block, (environ, tensors))


def block_product(env_block, right_blocks, chosen, ops, charges):

    def segment(total_sum, entries):
        left_block, right_block, bond_op, charge = entries
        source_tile = lax.dynamic_index_in_dim(chosen, charge + 1, 0, keepdims=False)
        contracted = jnp.dot(left_block, source_tile, preferred_element_type=jnp.float32).astype(
            jnp.bfloat16
        )
        shaped = contracted.reshape(contracted.shape[0], ops.shape[1], -1)
        applied = jnp.einsum(
            "asb,bc->asc", shaped, right_block, preferred_element_type=jnp.float32
        ).astype(jnp.bfloat16)
        final = jnp.einsum("asc,st->atc", applied, bond_op, preferred_element_type=jnp.float32)
        return (total_sum + final.reshape(total_sum.shape), None)

    start_sum = jnp.zeros((chosen.shape[1], chosen.shape[2]), jnp.float32)
    return lax.scan(segment, start_sum, (env_block, right_blocks, ops, charges))[0]


def keep_same(values):
    return values


def pair_with(environ, tensors, site_ops):
    first = env_update(environ, tensors[0], site_ops[0])
    return env_update(first, tensors[1], site_ops[1])


def picker(wanted_labels, pieces):
    sign_pair = jnp.array([-1, 1], jnp.int32)
    wanted = wanted_labels[:, None] + sign_pair[None, :]
    incoming_tiles, incoming_tags = pieces
    matches = (incoming_tags[None, None, :] == wanted[:, :, None]).astype(jnp.bfloat16)
    picked = jnp.einsum(
        "kst,tam->ksam", matches, incoming_tiles, preferred_element_type=jnp.float32
    )
    return picked.astype(jnp.bfloat16)


def on_device(
    theta,
    boundary_env,
    right_env,
    site_tensors,
    site_mpo,
    bond_ops,
    block_energy,
    sector_charge,
    block_len,
    channel_charge,
):
    section = lax.axis_index("site")
    site_count = lax.axis_size("site")
    tensors = site_tensors[0]
    site_ops = site_mpo[0]

    def update_pair(environ):
        return pair_with(environ, tensors, site_ops)

    state = boundary_env
    env_in = boundary_env
    for segment in range(site_count):
        state = lax.cond(section == segment, update_pair, keep_same, state)
        if segment + 1 < site_count:
            received = from_behind(state, "site", 1)
            is_next = section == segment + 1
            state = jnp.where(is_next, received, state)
            env_in = jnp.where(is_next, received, env_in)
    labels = sector_charge[0]
    live_rows = block_len[0]
    row_mask = jnp.arange(theta.shape[2], dtype=jnp.int32)[None, :] < live_rows[:, None]
    theta_m = theta[0] * row_mask[:, :, None].astype(jnp.bfloat16)
    other_labels = from_partner(labels, "charge", 0)
    for_other = picker(
        other_labels,
        (
            lax.all_gather(theta_m, "blk", axis=0, tiled=True),
            lax.all_gather(labels, "blk", axis=0, tiled=True),
        ),
    )
    partner = from_partner(for_other, "charge", 0)
    chosen_all = jnp.stack([partner[:, 0], theta_m, partner[:, 1]], axis=1)
    ops = bond_ops[0]

    def per_block(entries):
        return block_product(entries[0], entries[1], entries[2], ops, channel_charge)

    product = lax.map(per_block, (env_in, right_env[0], chosen_all))
    theta_f = theta_m.astype(jnp.float32)
    product = (
        product * row_mask[:, :, None].astype(jnp.float32)
        - block_energy[0][:, None, None] * theta_f
    )
    entries_count = NS * BS * M
    correlation, norm_theta = lax.psum(
        (jnp.sum(theta_f * product), jnp.sum(theta_f * theta_f)), ("blk", "charge")
    )
    rayleigh = correlation / norm_theta
    residual = product - rayleigh * theta_f
    residual_sq = lax.psum(jnp.sum(residual * residual), ("blk", "charge"))
    mean_sq = residual_sq / entries_count
    lanczos = (residual / jnp.sqrt(mean_sq + 1e-06)).astype(jnp.bfloat16)
    coefficients = jnp.stack([rayleigh, jnp.sqrt(mean_sq)])[None, :]
    return (state[None], lanczos[None], coefficients)


def solution(mesh):
    return jax.shard_map(
        on_device,
        mesh=mesh,
        in_specs=(
            P("site", ("blk", "charge"), None, None),
            P(("blk", "charge"), None, None, None),
            P("site", ("blk", "charge"), None, None, None),
            P("site", None, ("blk", "charge"), None, None, None),
            P("site", None, None, None, None, None),
            P("site", None, None, None),
            P("site", ("blk", "charge")),
            P("site", ("blk", "charge")),
            P("site", ("blk", "charge")),
            P(),
        ),
        out_specs=(
            P("site", ("blk", "charge"), None, None, None),
            P("site", ("blk", "charge"), None, None),
            P("site", None),
        ),
        check_vma=False,
    )
```

profile of v0, /device:TPU:97, one launch (start us, length us, event | category | flops | bytes accessed | tf_op | source)
XLA Modules:
  0.0 685.1 jit_solution(11959686821084895500)
XLA Ops:
  9.1 2.4 bitcast_multiply_fusion
  18.5 13.5 %all-reduce = s32[32]{0:T(128)S(1)} all-reduce(s32[32]{0:T(128)S(1)} %bitcast_dynamic-update-slice_fusion.1), channel_id=2, replica_groups=mesh['site'=4,'blk'=16,'charge'=2] {'blk'}, use_global_device_ids=true, to_apply=%add | all-reduce | flops 32 | bytes 256
  32.1 11.6 %collective-permute-done = bf16[2,18,128,128]{3,2,1,0:T(8,128)(2,1)S(1)} collective-permute-done((bf16[2,18,128,128]{3,2,1,0:T(8,128)(2,1)}, bf16[2,18,128,128]{3,2,1,0:T(8,128)(2,1)S(1)}, u32[]{:S(2)}, u32[]{:S(2)}) %collective-permute-start) | collective-permute-done | bytes 1179680 | tf_op jit(solution)/shard_map/ppermute | solution.py:14
  43.7 1.8 broadcast_select_fusion
  45.6 1.5 collective-permute-start.1
  47.0 77.2 %all-gather.3.cloned.1.call-done = bf16[32,128,2048]{2,1,0:T(8,128)(2,1)} async-done(((bf16[2,128,2048]{2,1,0:T(8,128)(2,1)}), bf16[32,128,2048]{2,1,0:T(8,128)(2,1)}) %all-gather.3.cloned.1.call-update) | async-done | bytes 16777232 | tf_op jit(solution)/shard_map/all_gather | solution.py:114
  124.2 26.1 %fusion.233 = bf16[2,2,128,2048]{3,1,2,0:T(2,128)(2,1)} fusion(bf16[32,128,2048]{2,1,0:T(8,128)(2,1)} %all-gather.3.cloned.1.call-done, s32[32]{0:T(128)S(1)} %all-reduce, s32[2,2]{1,0:T(2,128)S(1)} %broadcast_add_fusion), kind=kOutput, calls=%fused_computation.203 | convolution fusion | flops 68157568 | bytes 18874512 | tf_op jit(solution)/shard_map/kst,tam->ksam/dot_general | solution.py:71
  151.6 9.2 %collective-permute-start.2 = (bf16[2,18,128,128]{3,2,1,0:T(8,128)(2,1)S(1)}, bf16[2,18,128,128]{3,2,1,0:T(8,128)(2,1)}, u32[]{:S(2)}, u32[]{:S(2)}) collective-permute-start(bf16[2,18,128,128]{3,2,1,0:T(8,128)(2,1)S(1)} %get-tuple-element.589), channel_id=1, source_target_pairs={{0,32},{32,64},{64,96},{1,33},{33,65},{65,97},{2,34},{34,66},{66,9... | collective-permute-start | bytes 3538952 | tf_op jit(solution)/shard_map/ppermute | solution.py:14
  160.8 1.7 copy.99
  162.5 2.2 copy_multiply_fusion
  164.7 85.6 %collective-permute-done.2 = bf16[2,18,128,128]{3,2,1,0:T(8,128)(2,1)} collective-permute-done((bf16[2,18,128,128]{3,2,1,0:T(8,128)(2,1)S(1)}, bf16[2,18,128,128]{3,2,1,0:T(8,128)(2,1)}, u32[]{:S(2)}, u32[]{:S(2)}) %collective-permute-start.2) | collective-permute-done | bytes 1179680 | tf_op jit(solution)/shard_map/ppermute | solution.py:14
  250.4 2.7 select_select_fusion
  253.1 5.6 fusion.247
  258.6 7.1 %pad_maximum_fusion = bf16[2,3,128,2048]{3,1,2,0:T(4,128)(2,1)S(1)} fusion(bf16[2,1,128,2048]{3,1,2,0:T(2,128)(2,1)S(1)} %get-tuple-element.724, bf16[2,1,128,2048]{3,1,2,0:T(2,128)(2,1)S(1)} %copy_multiply_fusion, bf16[2,1,128,2048]{3,1,2,0:T(2,128)(2,1)S(1)} %get-tuple-element.723), kind=kLoop, calls=%fused_computation.198 | loop fusion | flops 9437184 | bytes 6291456 | tf_op jit(solution)/shard_map/stack | solution.py:119
  265.8 3.9 copy.100
  269.7 211.9 %while.113 = (s32[]{:T(128)}, f32[2,128,2048]{2,1,0:T(8,128)}, bf16[2,18,128,128]{3,2,1,0:T(8,128)(2,1)S(1)}, bf16[2,18,128,128]{3,2,1,0:T(8,128)(2,1)}, bf16[2,...) while((s32[]{:T(128)}, f32[2,128,2048]{2,1,0:T(8,128)}, ...), condition=%wide.region_27.28_spmd, body=%wide.region_24.27_spmd.sunk | while | flops 143654912 | bytes 23926256 | solution.py:125
  269.7 2.4 dynamic-slice_bitcast_fusion.5
  272.1 2.7 dynamic-slice_bitcast_fusion.6
  274.8 99.1 %while.114 = (s32[]{:T(128)}, f32[128,2048]{1,0:T(8,128)S(1)}, bf16[18,16,16]{1,2,0:T(8,128)(2,1)}, bf16[18,128,128]{2,1,0:T(8,128)(2,1)}, s32[18]{0:T(128)S(1)}...) while((s32[]{:T(128)}, f32[128,2048]{1,0:T(8,128)S(1)}, ...), condition=%wide.region_26.26_spmd.clone, body=%wide.region_25.25_spmd.clone.sunk | while | flops 143654912 | bytes 6886593 | solution.py:54
  375.6 2.4 dynamic-slice_bitcast_fusion.5
  378.0 2.7 dynamic-slice_bitcast_fusion.6
  380.7 99.1 %while.114 = (s32[]{:T(128)}, f32[128,2048]{1,0:T(8,128)S(1)}, bf16[18,16,16]{1,2,0:T(8,128)(2,1)}, bf16[18,128,128]{2,1,0:T(8,128)(2,1)}, s32[18]{0:T(128)S(1)}...) while((s32[]{:T(128)}, f32[128,2048]{1,0:T(8,128)S(1)}, ...), condition=%wide.region_26.26_spmd.clone, body=%wide.region_25.25_spmd.clone.sunk | while | flops 143654912 | bytes 6886593 | solution.py:54
  382.8 1.4 fusion.325
  399.3 1.4 fusion.325
  415.8 1.4 fusion.325
  481.5 3.8 fusion.238
  485.3 68.7 %all-reduce.1 = (f32[]{:T(128)}, f32[]{:T(128)}) all-reduce(f32[]{:T(128)} %get-tuple-element.594, f32[]{:T(128)} %get-tuple-element.593), channel_id=1, replica_groups=mesh['site'=4,'blk'=16,'charge'=2] {'blk','charge'}, use_global_device_ids=true, to_apply=%region_29.30 | all-reduce | flops 2 | bytes 16 | tf_op jit(solution)/shard_map/psum | solution.py:132
  555.4 3.3 multiply_reduce_fusion
  558.7 48.6 %conditional.7 = (bf16[1,2,18,128,128]{4,3,2,1,0:T(8,128)(2,1)}) conditional(s32[]{:T(128)} %convert_element_type.194, (bf16[2,18,128,128]{3,2,1,0:T(8,128)(2,1)S(1)}) %tuple.289, (bf16[2,2,4,128,128]{3,4,2,1,0:T(8,128)(2,1)}, bf16[2,18,18,4,4]{1,2,4,3,0:T(8,128)(2,1)}, bf16[2,18,128,128]{3,2,1,0:T(8,128)(2,1)S(1)}) %tuple.290), branch_computations={%region_18.19_spmd, %region_19.24_spmd} | conditional | flops 1553006592 | bytes 31303274 | solution.py:100
  558.7 1.9 slice_bitcast_fusion.12
  560.6 1.6 slice_bitcast_fusion.14
  562.5 21.7 %while.109 = (s32[]{:T(128)}, bf16[2,18,128,128]{2,3,1,0:T(8,128)(2,1)S(1)}, bf16[2,4,128,128]{2,3,1,0:T(8,128)(2,1)}, bf16[2,18,128,128]{3,2,1,0:T(8,128)(2,1)S(1)}, bf16[18,18,4,4]{0,1,3,2:T(8,128)(2,1)}, /*index=5*/s32[]{:T(128)}) while((s32[]{:T(128)}, bf16[2,18,128,128]{2,3,1,0:T(8,128)(2,1)S(1)}, bf16[2,4,128,128]{2,3,1,0:T(8,128)(2,1)}, ...), condition=%wide.region_21.21_spmd, body=%wide.region_20.20_spmd.sunk | while | flops 776503296 | bytes 12768005 | solution.py:35
  562.7 1.7 convert_bitcast_fusion.16
  564.4 7.2 %fusion.333 = bf16[18,4,128,128]{2,0,1,3:T(8,128)(2,1)S(1)} fusion(bf16[18,4,128,128,1]{2,3,0,1,4:T(8,128)(2,1)S(1)} %convert_bitcast_fusion.16, bf16[18,18,4,4]{0,1,3,2:T(8,128)(2,1)S(1)} %copy-done.20), kind=kOutput, calls=%fused_computation.133.clone.1 | convolution fusion | flops 171048960 | bytes 4728960 | tf_op jit(solution)/shard_map/cond/branch_1_fun/while/body/eval_jaxpr/wvts,wsac->vtac/dot_general | solution.py:28
  571.6 1.7 fusion.334
  573.4 1.7 convert_bitcast_fusion.16
  575.2 7.2 %fusion.333 = bf16[18,4,128,128]{2,0,1,3:T(8,128)(2,1)S(1)} fusion(bf16[18,4,128,128,1]{2,3,0,1,4:T(8,128)(2,1)S(1)} %convert_bitcast_fusion.16, bf16[18,18,4,4]{0,1,3,2:T(8,128)(2,1)S(1)} %copy-done.20), kind=kOutput, calls=%fused_computation.133.clone.1 | convolution fusion | flops 171048960 | bytes 4728960 | tf_op jit(solution)/shard_map/cond/branch_1_fun/while/body/eval_jaxpr/wvts,wsac->vtac/dot_general | solution.py:28
  582.4 1.7 fusion.334
  584.4 21.3 %while.110 = (s32[]{:T(128)}, bf16[2,18,128,128]{2,3,1,0:T(8,128)(2,1)S(1)}, bf16[2,4,128,128]{2,3,1,0:T(8,128)(2,1)}, bf16[2,18,128,128]{2,3,1,0:T(8,128)(2,1)S...) while((s32[]{:T(128)}, bf16[2,18,128,128]{2,3,1,0:T(8,128)(2,1)S(1)}, ...), condition=%wide.region_23.23_spmd, body=%wide.region_22.22_spmd.sunk | while | flops 776503296 | bytes 12726505 | solution.py:35
  584.4 1.7 convert_bitcast_fusion.17
  586.1 7.2 %fusion.341 = bf16[18,4,128,128]{2,0,1,3:T(8,128)(2,1)S(1)} fusion(bf16[18,4,128,128,1]{2,3,0,1,4:T(8,128)(2,1)S(1)} %convert_bitcast_fusion.17, bf16[18,18,4,4]{0,1,3,2:T(8,128)(2,1)S(1)} %get-tuple-element.1151), kind=kOutput, calls=%fused_computation.153.clone.1 | convolution fusion | flops 171048960 | bytes 4728960 | tf_op jit(solution)/shard_map/cond/branch_1_fun/while/body/eval_jaxpr/wvts,wsac->vtac/dot_general | solution.py:28
  593.3 1.7 fusion.342
  595.1 1.7 convert_bitcast_fusion.17
  596.8 7.2 %fusion.341 = bf16[18,4,128,128]{2,0,1,3:T(8,128)(2,1)S(1)} fusion(bf16[18,4,128,128,1]{2,3,0,1,4:T(8,128)(2,1)S(1)} %convert_bitcast_fusion.17, bf16[18,18,4,4]{0,1,3,2:T(8,128)(2,1)S(1)} %get-tuple-element.1151), kind=kOutput, calls=%fused_computation.153.clone.1 | convolution fusion | flops 171048960 | bytes 4728960 | tf_op jit(solution)/shard_map/cond/branch_1_fun/while/body/eval_jaxpr/wvts,wsac->vtac/dot_general | solution.py:28
  604.0 1.7 fusion.342
  605.7 1.4 copy.177
  607.4 65.9 %psum.23 = f32[]{:T(128)} all-reduce(f32[]{:T(128)} %multiply_reduce_fusion), channel_id=1, replica_groups=mesh['site'=4,'blk'=16,'charge'=2] {'blk','charge'}, use_global_device_ids=true, to_apply=%region_33.34 | all-reduce | flops 1 | bytes 8 | tf_op jit(solution)/shard_map/psum | solution.py:137
  674.0 3.3 fusion.240
  (257 shorter events, 158.0 us)
Async XLA Ops:
  7.2 4.4 copy-start.18
  7.2 5.4 copy-start.17
  7.2 117.0 %all-gather.3.cloned.1.call-start = ((), (), s32[]{:S(2)}) async-start(), calls=%async_computation | async-start | bytes 17825792 | tf_op jit(solution)/shard_map/all_gather | solution.py:114
  8.6 0.5 copy-start.21
  9.1 4.5 copy-start.2
  13.6 2.3 copy-start.26
  13.6 3.4 copy-start.28
  13.6 18.4 %copy-start.25 = (s32[2]{0:T(128)S(1)}, s32[2]{0:T(128)}, u32[]{:S(2)}) copy-start(s32[2]{0:T(128)} %constant.168.clone) | copy-start | bytes 28
  14.7 29.0 %collective-permute-start = (bf16[2,18,128,128]{3,2,1,0:T(8,128)(2,1)}, bf16[2,18,128,128]{3,2,1,0:T(8,128)(2,1)S(1)}, u32[]{:S(2)}, u32[]{:S(2)}) collective-permute-start(bf16[2,18,128,128]{3,2,1,0:T(8,128)(2,1)} %get-tuple-element.585), channel_id=1, source_target_pairs={{0,32},{32,64},{64,96},{1,33},{33,65},{65,97},{2,34},{34,66},{66,9... | collective-permute-start | bytes 3538952 | tf_op jit(solution)/shard_map/ppermute | solution.py:14
  16.0 16.0 %collective-permute-start.3 = (s32[2]{0:T(128)S(1)}, s32[2]{0:T(128)S(1)}, u32[]{:S(2)}, u32[]{:S(2)}) collective-permute-start(s32[2]{0:T(128)S(1)} %bitcast.620), channel_id=1, source_target_pairs={{0,1},{1,0},{2,3},{3,2},{4,5},{5,4},{6,7},{7,6},{8,9},{9,8},{10,11... | collective-permute-start | bytes 32 | tf_op jit(solution)/shard_map/ppermute | solution.py:18
  43.7 1.8 copy-start.8
  45.6 105.5 %collective-permute-start.1 = (bf16[2,18,128,128]{3,2,1,0:T(8,128)(2,1)S(1)}, bf16[2,18,128,128]{3,2,1,0:T(8,128)(2,1)}, u32[]{:S(2)}, u32[]{:S(2)}) collective-permute-start(bf16[2,18,128,128]{3,2,1,0:T(8,128)(2,1)S(1)} %get-tuple-element.587), channel_id=1, source_target_pairs={{0,32},{32,64},{64,96},{1,33},{33,65},{65,97},{2,34},{34,66},{66,9... | collective-permute-start | bytes 3538952 | tf_op jit(solution)/shard_map/ppermute | solution.py:14
  150.3 102.7 %collective-permute-start.4 = (bf16[2,2,128,2048]{3,1,2,0:T(2,128)(2,1)}, bf16[2,2,128,2048]{3,1,2,0:T(2,128)(2,1)}, u32[]{:S(2)}, u32[]{:S(2)}) collective-permute-start(bf16[2,2,128,2048]{3,1,2,0:T(2,128)(2,1)} %fusion.233), channel_id=1, source_target_pairs={{0,1},{1,0},{2,3},{3,2},{4,5},{5,4},{6,7},{7,6},{8,9},{9,8},{10,11... | collective-permute-start | bytes 6291464 | tf_op jit(solution)/shard_map/ppermute | solution.py:18
  151.2 11.3 %copy-start = (bf16[1,2,128,2048]{3,2,1,0:T(8,128)(2,1)S(1)}, bf16[1,2,128,2048]{3,2,1,0:T(8,128)(2,1)}, u32[]{:S(2)}) copy-start(bf16[1,2,128,2048]{3,2,1,0:T(8,128)(2,1)} %param.39) | copy-start | bytes 3145732
  151.2 11.3 %copy-start.22 = (bf16[2,128]{1,0:T(2,128)(2,1)S(1)}, bf16[2,128]{1,0:T(2,128)(2,1)}, u32[]{:S(2)}) copy-start(bf16[2,128]{1,0:T(2,128)(2,1)} %copy-done.21) | copy-start | bytes 1540
  151.6 98.7 %collective-permute-start.2 = (bf16[2,18,128,128]{3,2,1,0:T(8,128)(2,1)S(1)}, bf16[2,18,128,128]{3,2,1,0:T(8,128)(2,1)}, u32[]{:S(2)}, u32[]{:S(2)}) collective-permute-start(bf16[2,18,128,128]{3,2,1,0:T(8,128)(2,1)S(1)} %get-tuple-element.589), channel_id=1, source_target_pairs={{0,32},{32,64},{64,96},{1,33},{33,65},{65,97},{2,34},{34,66},{66,9... | collective-permute-start | bytes 3538952 | tf_op jit(solution)/shard_map/ppermute | solution.py:14
  162.5 87.9 %copy-start.9 = (bf16[2,18,128,128]{3,2,1,0:T(8,128)(2,1)S(1)}, bf16[2,18,128,128]{3,2,1,0:T(8,128)(2,1)}, u32[]{:S(2)}) copy-start(bf16[2,18,128,128]{3,2,1,0:T(8,128)(2,1)} %copy-done.8) | copy-start | bytes 3538948
  265.8 3.9 copy-start.27
  269.7 211.9 %copy-start.23 = (f32[2,128]{1,0:T(2,128)S(1)}, f32[2,128]{1,0:T(2,128)}, u32[]{:S(2)}) copy-start(f32[2,128]{1,0:T(2,128)} %get-tuple-element.727) | copy-start | bytes 3076
  269.7 211.9 %copy-start.24 = (f32[1,2]{1,0:T(1,128)S(1)}, f32[1,2]{1,0:T(1,128)}, u32[]{:S(2)}) copy-start(f32[1,2]{1,0:T(1,128)} %param.45) | copy-start | bytes 28
  269.7 5.2 copy-start.4
  374.0 1.6 copy-start.5
  375.6 5.1 copy-start.4
  479.9 1.6 copy-start.5
  481.5 73.8 %copy-start.1 = (bf16[1,2,128,2048]{3,2,1,0:T(8,128)(2,1)S(1)}, bf16[1,2,128,2048]{3,2,1,0:T(8,128)(2,1)}, u32[]{:S(2)}) copy-start(bf16[1,2,128,2048]{3,2,1,0:T(8,128)(2,1)} %param.39) | copy-start | bytes 3145732
  481.5 73.8 %copy-start.3 = (bf16[2,18,128,128]{3,2,1,0:T(8,128)(2,1)S(1)}, bf16[2,18,128,128]{3,2,1,0:T(8,128)(2,1)}, u32[]{:S(2)}) copy-start(bf16[2,18,128,128]{3,2,1,0:T(8,128)(2,1)} %get-tuple-element.726) | copy-start | bytes 3538948
  562.7 1.7 copy-start.20
  564.4 7.2 %copy-start.14 = (bf16[2,4,128,128]{2,3,1,0:T(8,128)(2,1)S(1)}, bf16[2,4,128,128]{2,3,1,0:T(8,128)(2,1)}, u32[]{:S(2)}) copy-start(bf16[2,4,128,128]{2,3,1,0:T(8,128)(2,1)} %get-tuple-element.1131) | copy-start | bytes 786436 | tf_op jit(solution)/shard_map/cond/branch_1_fun/while
  573.4 1.7 copy-start.20
  575.2 7.2 %copy-start.14 = (bf16[2,4,128,128]{2,3,1,0:T(8,128)(2,1)S(1)}, bf16[2,4,128,128]{2,3,1,0:T(8,128)(2,1)}, u32[]{:S(2)}) copy-start(bf16[2,4,128,128]{2,3,1,0:T(8,128)(2,1)} %get-tuple-element.1131) | copy-start | bytes 786436 | tf_op jit(solution)/shard_map/cond/branch_1_fun/while
  586.1 7.2 %copy-start.11 = (bf16[2,4,128,128]{2,3,1,0:T(8,128)(2,1)S(1)}, bf16[2,4,128,128]{2,3,1,0:T(8,128)(2,1)}, u32[]{:S(2)}) copy-start(bf16[2,4,128,128]{2,3,1,0:T(8,128)(2,1)} %get-tuple-element.1149) | copy-start | bytes 786436 | tf_op jit(solution)/shard_map/cond/branch_1_fun/while
  596.7 7.2 %copy-start.11 = (bf16[2,4,128,128]{2,3,1,0:T(8,128)(2,1)S(1)}, bf16[2,4,128,128]{2,3,1,0:T(8,128)(2,1)}, u32[]{:S(2)}) copy-start(bf16[2,4,128,128]{2,3,1,0:T(8,128)(2,1)} %get-tuple-element.1149) | copy-start | bytes 786436 | tf_op jit(solution)/shard_map/cond/branch_1_fun/while
Sparse Core Ops, SparseCore 0:
  11.7 112.4 all-gather.2
where the time goes:
time: 698 us; the launch traced here: 685 us
  waiting for transfers between devices  174 us (25%)
  matrix products  161 us (23%)
  blocking collectives  148 us (21%)
  local copies, waits for them, and re-layouts  62.4 us (9%)
  other arithmetic  56 us (8%)
  loops' own time  52.4 us (8%)
  between operations  17.4 us (2%)
  starting transfers between devices  13.8 us (2%)
    ppermute x3, waiting for transfers between devices, from_behind(): return lax.ppermute(block, axis, route)  97.3 us
    all_gather x1, waiting for transfers between devices, on_device(): lax.all_gather(theta_m, 'blk', axis=0, tiled=True)  77.2 us
    psum x1, blocking collectives, on_device(): lax.psum((jnp.sum(theta_f * product), jnp.sum(theta_f * theta_f)), ('blk'...  68.7 us
    psum x1, blocking collectives, on_device(): residual_sq = lax.psum(jnp.sum(residual * residual), ('blk', 'charge'))  65.9 us
    another operation x2, loops' own time, block_product(): lax.scan(segment, start_sum, (env_block, right_blocks, ops, charges))[0]  51.2 us
    dot_general x36, matrix products, segment(): jnp.dot(left_block, source_tile, preferred_element_type=jnp.float32)  48.7 us
    dot_general x36, matrix products, segment(): jnp.einsum('asc,st->atc', applied, bond_op, preferred_element_type=jnp.fl...  43.4 us
    dot_general x4, matrix products, one_block(): jnp.einsum('wvts,wsac->vtac', site_op, left_part, preferred_element_type=...  28.8 us
  transfers between devices with their start and end apart: 6, of which 3 were waited for; matrix products, arithmetic and copies ran while one was open for 6% of the time, Pallas kernels for 0%

commit v1 on v0

v1 whole, which is shorter than its diff:
```python
import jax
import jax.numpy as jnp
from jax import lax
from jax.experimental import pallas as pl
from jax.experimental.pallas import tpu as pltpu
from jax.sharding import PartitionSpec as P

BS = 128
PH = 4
WCH = 18
WP = 24
PP = 16
M = 2048
NS = 64
SEC = 4
NBLK = 16
NDEV = 32
F32 = jnp.float32
BF16 = jnp.bfloat16
MESH = pl.DeviceIdType.MESH
VMEM_LIMIT = 64 * 1024 * 1024 - 64 * 1024
CH = 8


def mm(a, b):
    return jnp.dot(a, b, preferred_element_type=F32)


def env_site(a_ref, w_ref, l_ref, m_ref, at_ref, out_ref):
    for t in range(PH):
        at_ref[:, t * BS : (t + 1) * BS] = a_ref[t].T
    a_cat = jnp.concatenate([a_ref[s] for s in range(PH)], axis=1)
    w2 = w_ref[:, : PH * WP]

    def chunk(ci, carry):
        base = pl.multiple_of(ci * (CH * WP), CH * WP)
        left = mm(l_ref[pl.ds(base, CH * WP), :].astype(BF16), a_cat)
        for j in range(0, CH, 2):
            sides = []
            for e in (j, j + 1):
                rows = left[e * WP : (e + 1) * WP]
                sides.append(
                    jnp.concatenate([rows[:, s * BS : (s + 1) * BS] for s in range(PH)], axis=0)
                )
            mixed = mm(w2, jnp.concatenate(sides, axis=1).astype(BF16))
            for e in range(2):
                start = pl.multiple_of((ci * CH + j + e) * (PH * WCH), 8)
                m_ref[pl.ds(start, PH * WCH), :] = mixed[: PH * WCH, e * BS : (e + 1) * BS]
        return carry

    lax.fori_loop(0, BS // CH, chunk, 0)

    def channels(vi, carry):
        sides = []
        for e in range(2):
            sides.append(
                jnp.concatenate(
                    [
                        m_ref[pl.ds(t * WCH + vi * 2 + e, BS, stride=PH * WCH), :]
                        for t in range(PH)
                    ],
                    axis=0,
                )
            )
        new = mm(at_ref[...], jnp.concatenate(sides, axis=1).astype(BF16))
        for e in range(2):
            one = new[:, e * BS : (e + 1) * BS]
            out_ref[vi * 2 + e] = one.astype(BF16)
            l_ref[pl.ds(vi * 2 + e, BS, stride=WP), :] = one
        return carry

    lax.fori_loop(0, WCH // 2, channels, 0)


def load_env(env_ref, l_ref, slot_ref):
    l_ref[...] = jnp.zeros_like(l_ref)

    def one(v, carry):
        block = env_ref[v]
        slot_ref[v] = block
        l_ref[pl.ds(v, BS, stride=WP), :] = block.astype(F32)
        return carry

    lax.fori_loop(0, WCH, one, 0)


def exchange_kernel(
    theta_ref,
    lab_ref,
    tens_ref,
    w2_ref,
    benv_ref,
    partner_ref,
    envin_ref,
    envout_ref,
    recv1,
    send2,
    lab_all,
    inv,
    lab_s,
    inv_s,
    tens,
    w2,
    left,
    mixed,
    at,
    envs,
    lab_send,
    lab_recv,
    one_send,
    one_recv,
    two_send,
    two_recv,
    ten_send,
    ten_recv,
    w_send,
    w_recv,
    local,
):
    z = lax.axis_index("site")
    blk = lax.axis_index("blk")
    core = lax.axis_index("charge")
    me = blk * 2 + core

    barrier = pltpu.get_barrier_semaphore()

    def greet(off, carry):
        dev = lax.rem(me + off, NDEV)
        pl.semaphore_signal(
            barrier,
            inc=1,
            device_id={"blk": lax.div(dev, 2), "charge": lax.rem(dev, 2)},
            device_id_type=MESH,
        )
        return carry

    lax.fori_loop(1, NDEV, greet, 0)
    for off in range(1, SEC):
        pl.semaphore_signal(
            barrier,
            inc=1,
            device_id={"site": lax.rem(z + off, SEC)},
            device_id_type=MESH,
        )
    pl.semaphore_wait(barrier, NDEV - 1 + SEC - 1)

    def labels_to(off, peer):
        dev = lax.rem(me + off, NDEV)
        return pltpu.make_async_remote_copy(
            src_ref=lab_ref,
            dst_ref=lab_all.at[me],
            send_sem=lab_send.at[off],
            recv_sem=lab_recv.at[peer],
            device_id={"blk": lax.div(dev, 2), "charge": lax.rem(dev, 2)},
            device_id_type=MESH,
        )

    def piece_to(off, peer):
        dev = lax.rem(blk + off, NBLK)
        return pltpu.make_async_remote_copy(
            src_ref=theta_ref.at[:, :, pl.ds(pl.multiple_of(dev * BS, BS), BS)],
            dst_ref=recv1.at[pl.ds(1 + 2 * blk, 2)],
            send_sem=one_send.at[off],
            recv_sem=one_recv.at[peer],
            device_id={"blk": dev},
            device_id_type=MESH,
        )

    def picked_to(off, peer):
        dev = lax.rem(blk + off, NBLK)
        return pltpu.make_async_remote_copy(
            src_ref=send2.at[dev],
            dst_ref=partner_ref.at[blk],
            send_sem=two_send.at[off],
            recv_sem=two_recv.at[peer],
            device_id={"blk": dev, "charge": 1 - core},
            device_id_type=MESH,
        )

    def tensors_to(off, sec):
        return pltpu.make_async_remote_copy(
            src_ref=tens_ref,
            dst_ref=tens.at[z],
            send_sem=ten_send.at[off],
            recv_sem=ten_recv.at[sec],
            device_id={"site": lax.rem(z + off, SEC)},
            device_id_type=MESH,
        )

    def mixer_to(off, sec):
        return pltpu.make_async_remote_copy(
            src_ref=w2_ref,
            dst_ref=w2.at[z],
            send_sem=w_send.at[off],
            recv_sem=w_recv.at[sec],
            device_id={"site": lax.rem(z + off, SEC)},
            device_id_type=MESH,
        )

    def loop(low, high, body):
        def step(i, carry):
            body(i)
            return carry

        lax.fori_loop(low, high, step, 0)

    loop(1, NDEV, lambda off: labels_to(off, me).start())
    loop(1, NBLK, lambda off: piece_to(off, blk).start())
    for off in (1, 3, 2):

        @pl.when(z + off < SEC)
        def _():
            mixer_to(off, z).start()
            tensors_to(off, z).start()

    own_piece = pltpu.make_async_copy(
        theta_ref.at[:, :, pl.ds(pl.multiple_of(blk * BS, BS), BS)],
        recv1.at[pl.ds(1 + 2 * blk, 2)],
        local.at[0],
    )
    own_piece.start()
    own_tens = pltpu.make_async_copy(tens_ref, tens.at[z], local.at[1])
    own_tens.start()
    own_w2 = pltpu.make_async_copy(w2_ref, w2.at[z], local.at[2])
    own_w2.start()
    recv1[0] = jnp.zeros((BS, BS), BF16)
    lab_all[me] = lab_ref[...]
    for k in range(2):
        load_env(benv_ref.at[k], left.at[k], envs.at[0, k])

    loop(1, NDEV, lambda off: labels_to(off, lax.rem(me + off, NDEV)).wait_recv())
    total = jnp.zeros((8, BS), jnp.int32)
    for i in range(NBLK):
        total = total + lab_all[2 * i + core]
    inv[...] = total
    to_s0 = pltpu.make_async_copy(lab_all, lab_s, local.at[3])
    to_s0.start()
    to_s1 = pltpu.make_async_copy(inv, inv_s, local.at[4])
    to_s1.start()
    to_s0.wait()
    to_s1.wait()
    own_piece.wait()
    loop(1, NBLK, lambda off: piece_to(off, lax.rem(blk + off, NBLK)).wait_recv())

    def pick(dev):
        for k in range(2):
            label = lab_s[2 * dev + (1 - core), 0, 126 + k]
            for gi in range(2):
                send2[dev, 2 * k + gi] = recv1[inv_s[0, label + 2 * gi]]

    loop(0, NBLK, pick)
    loop(0, NBLK, lambda off: picked_to(off, blk).start())

    own_tens.wait()
    own_w2.wait()

    def stage(sec):
        @pl.when(sec < z)
        def _():
            mixer_to(1, sec).wait_recv()
            tensors_to(1, sec).wait_recv()

        slot = jnp.where(sec < z, 0, 1)

        def site(q):
            i, k = lax.div(q, 2), lax.rem(q, 2)
            env_site(
                tens.at[sec, i, k], w2.at[sec, i], left.at[k], mixed, at, envs.at[slot, k]
            )

        loop(0, 4, site)

    loop(0, z + 1, stage)
    out0 = pltpu.make_async_copy(envs.at[0], envin_ref, local.at[5])
    out1 = pltpu.make_async_copy(envs.at[1], envout_ref, local.at[6])
    out0.start()
    out1.start()

    loop(0, NBLK, lambda off: picked_to(off, lax.rem(blk + off, NBLK)).wait_recv())
    loop(1, NDEV, lambda off: labels_to(off, me).wait_send())
    loop(1, NBLK, lambda off: piece_to(off, blk).wait_send())
    loop(0, NBLK, lambda off: picked_to(off, blk).wait_send())
    for off in (1, 3, 2):

        @pl.when(z + off < SEC)
        def _():
            mixer_to(off, z).wait_send()
            tensors_to(off, z).wait_send()

    out0.wait()
    out1.wait()


def exchange(theta_m, lab_row, tensors, w2, benv):
    hbm = pl.BlockSpec(memory_space=pl.ANY)
    vmem = pl.BlockSpec(memory_space=pltpu.VMEM)
    env_shape = jax.ShapeDtypeStruct((2, WCH, BS, BS), BF16)
    dma = pltpu.SemaphoreType.DMA
    return pl.pallas_call(
        exchange_kernel,
        out_shape=(jax.ShapeDtypeStruct((NBLK, 4, BS, BS), BF16), env_shape, env_shape),
        in_specs=[hbm, vmem, hbm, hbm, vmem],
        out_specs=(hbm, hbm, hbm),
        scratch_shapes=[
            pltpu.VMEM((NDEV + 1, BS, BS), BF16),
            pltpu.VMEM((NBLK, 4, BS, BS), BF16),
            pltpu.VMEM((NDEV, 8, BS), jnp.int32),
            pltpu.VMEM((8, BS), jnp.int32),
            pltpu.SMEM((NDEV, 8, BS), jnp.int32),
            pltpu.SMEM((8, BS), jnp.int32),
            pltpu.VMEM((SEC, 2, 2, PH, BS, BS), BF16),
            pltpu.VMEM((SEC, 2, 80, BS), BF16),
            pltpu.VMEM((2, BS * WP, BS), F32),
            pltpu.VMEM((BS * PH * WCH, BS), F32),
            pltpu.VMEM((BS, PH * BS), BF16),
            pltpu.VMEM((2, 2, WCH, BS, BS), BF16),
            dma((NDEV,)),
            dma((NDEV,)),
            dma((NBLK,)),
            dma((NBLK,)),
            dma((NBLK,)),
            dma((NBLK,)),
            dma((SEC,)),
            dma((SEC,)),
            dma((SEC,)),
            dma((SEC,)),
            dma((8,)),
        ],
        compiler_params=pltpu.CompilerParams(
            collective_id=0, has_side_effects=True, vmem_limit_bytes=VMEM_LIMIT
        ),
        name="exchange_chain",
    )(theta_m, lab_row, tensors, w2, benv)


def build_kron(ops_ref, kron):
    big = (PP * PP, PP)
    rep = (
        lax.div(lax.broadcasted_iota(jnp.int32, big, 0), PP)
        == lax.broadcasted_iota(jnp.int32, big, 1)
    ).astype(F32).astype(BF16)
    wide = (PP, PP * PP)
    rep_t = (
        lax.div(lax.broadcasted_iota(jnp.int32, wide, 1), PP)
        == lax.broadcasted_iota(jnp.int32, wide, 0)
    ).astype(F32).astype(BF16)
    full = (PP * PP, PP * PP)
    same = lax.rem(lax.broadcasted_iota(jnp.int32, full, 0), PP) == lax.rem(
        lax.broadcasted_iota(jnp.int32, full, 1), PP
    )

    def one(w, carry):
        rows = mm(rep, ops_ref[w]).astype(BF16)
        kron[w] = jnp.where(same, mm(rows, rep_t), 0.0).astype(BF16)
        return carry

    lax.fori_loop(0, WCH, one, 0)


def block_product(charge_of, kron, tiles, env_ref, right_ref, mixed, states, acc):
    def pair(wi, carry):
        for e in range(2):
            w = wi * 2 + e
            c = charge_of(w)
            k = kron[w]
            for g in range(4):
                sides = []
                for h in range(2):
                    r0 = (g * 2 + h) * 16
                    sides.append(tiles[c, :, r0 : r0 + 16, :].reshape(PP * 16, BS))
                part = mm(k, jnp.concatenate(sides, axis=1)).astype(BF16)
                for h in range(2):
                    r0 = (g * 2 + h) * 16
                    mixed[:, r0 : r0 + 16, :] = part[:, h * BS : (h + 1) * BS].reshape(PP, 16, BS)
            env = env_ref[w]
            for t in range(0, PP, 2):
                part = mm(env, jnp.concatenate([mixed[t], mixed[t + 1]], axis=1)).astype(BF16)
                states[e, t] = part[:, :BS]
                states[e, t + 1] = part[:, BS:]
        right = right_ref[pl.ds(wi * 2, 2)].reshape(2 * BS, BS)
        for t in range(0, PP, 4):
            both = jnp.concatenate(
                [states[e, t : t + 4].reshape(4 * BS, BS) for e in range(2)], axis=1
            )
            acc[t : t + 4] += mm(both, right).reshape(4, BS, BS)
        return carry

    acc[...] = jnp.zeros_like(acc)
    lax.fori_loop(0, WCH // 2, pair, 0)


def product_kernel(
    charge_ref,
    len_ref,
    energy_ref,
    partner_ref,
    theta_ref,
    env_ref,
    right_ref,
    ops_ref,
    lanczos_ref,
    coef_ref,
    tiles,
    kron,
    mixed,
    states,
    acc,
    mine,
    stats,
    stat_send,
    stat_recv,
    local,
):
    blk = lax.axis_index("blk")
    core = lax.axis_index("charge")
    me = blk * 2 + core
    barrier = pltpu.get_barrier_semaphore()

    def loop(low, high, body):
        def step(i, carry):
            body(i)
            return carry

        lax.fori_loop(low, high, step, 0)

    def greet(off):
        dev = lax.rem(me + off, NDEV)
        pl.semaphore_signal(
            barrier,
            inc=1,
            device_id={"blk": lax.div(dev, 2), "charge": lax.rem(dev, 2)},
            device_id_type=MESH,
        )

    def tile_copy(s):
        out = []
        for k in range(2):
            for gi in range(2):
                out.append(
                    pltpu.make_async_copy(
                        partner_ref.at[s, 2 * k + gi], tiles.at[k, 2 * gi, s], local.at[2 * k + gi, s]
                    )
                )
            out.append(
                pltpu.make_async_copy(
                    theta_ref.at[k, :, pl.ds(pl.multiple_of(s * BS, BS), BS)],
                    tiles.at[k, 1, s],
                    local.at[4 + k, s],
                )
            )
        return out

    loop(0, PP, lambda s: [copy.start() for copy in tile_copy(s)])
    loop(1, NDEV, greet)
    build_kron(ops_ref, kron)
    loop(0, PP, lambda s: [copy.wait() for copy in tile_copy(s)])

    for k in range(2):
        block_product(
            lambda w: charge_ref[w] + 1,
            kron,
            tiles.at[k],
            env_ref.at[k],
            right_ref.at[k],
            mixed,
            states,
            acc.at[k],
        )

    rows = lax.broadcasted_iota(jnp.int32, (BS, BS), 0)
    zero = jnp.zeros((8, BS), F32)

    def fold(x):
        return jnp.sum(x.reshape(16, 8, BS), axis=0)

    def sums_one(t, carry):
        cor, nor = carry
        for k in range(2):
            th = tiles[k, 1, t].astype(F32)
            p = jnp.where(rows < len_ref[k], acc[k, t], 0.0) - energy_ref[k] * th
            acc[k, t] = p
            cor = cor + fold(p * th)
            nor = nor + fold(th * th)
        return cor, nor

    cor, nor = lax.fori_loop(0, PP, sums_one, (zero, zero))

    def everywhere(x):
        return jnp.broadcast_to(
            jnp.sum(jnp.sum(x, axis=0, keepdims=True), axis=1, keepdims=True), (1, BS)
        )

    cor, nor = everywhere(cor), everywhere(nor)
    rho = jnp.where(nor > 0, cor / jnp.where(nor > 0, nor, 1.0), 0.0)

    def sums_two(t, carry):
        sq, cross = carry
        for k in range(2):
            th = tiles[k, 1, t].astype(F32)
            r = acc[k, t] - rho * th
            sq = sq + fold(r * r)
            cross = cross + fold(r * th)
        return sq, cross

    sq, cross = lax.fori_loop(0, PP, sums_two, (zero, zero))
    mine[0:1] = cor
    mine[1:2] = nor
    mine[2:3] = everywhere(sq)
    mine[3:4] = everywhere(cross)
    mine[4:5] = rho
    stats[me] = mine[...]

    def stat_to(off, peer):
        dev = lax.rem(me + off, NDEV)
        return pltpu.make_async_remote_copy(
            src_ref=mine,
            dst_ref=stats.at[me],
            send_sem=stat_send.at[off],
            recv_sem=stat_recv.at[peer],
            device_id={"blk": lax.div(dev, 2), "charge": lax.rem(dev, 2)},
            device_id_type=MESH,
        )

    pl.semaphore_wait(barrier, NDEV - 1)
    loop(1, NDEV, lambda off: stat_to(off, me).start())
    loop(1, NDEV, lambda off: stat_to(off, lax.rem(me + off, NDEV)).wait_recv())

    cor_all = jnp.zeros((1, BS), F32)
    nor_all = jnp.zeros((1, BS), F32)
    for i in range(NDEV):
        cor_all = cor_all + stats[i, 0:1]
        nor_all = nor_all + stats[i, 1:2]
    ray = cor_all / nor_all
    res = jnp.zeros((1, BS), F32)
    for i in range(NDEV):
        gap = stats[i, 4:5] - ray
        res = res + (stats[i, 2:3] + gap * (2.0 * stats[i, 3:4] + gap * stats[i, 1:2]))
    mean_sq = jnp.maximum(res, 0.0) / (NS * BS * M)
    scale = 1.0 / jnp.sqrt(mean_sq + 1e-06)

    def finish(t):
        for k in range(2):
            th = tiles[k, 1, t].astype(F32)
            lanczos_ref[k, :, pl.ds(pl.multiple_of(t * BS, BS), BS)] = (
                (acc[k, t] - ray * th) * scale
            ).astype(BF16)

    loop(0, PP, finish)
    coef_ref[...] = jnp.zeros_like(coef_ref)
    coef_ref[0:1] = ray
    coef_ref[1:2] = jnp.sqrt(mean_sq)
    loop(1, NDEV, lambda off: stat_to(off, me).wait_send())


def product(charges, lens, energy, partner, theta_m, env_in, right, ops_t):
    hbm = pl.BlockSpec(memory_space=pl.ANY)
    vmem = pl.BlockSpec(memory_space=pltpu.VMEM)
    smem = pl.BlockSpec(memory_space=pltpu.SMEM)
    dma = pltpu.SemaphoreType.DMA
    return pl.pallas_call(
        product_kernel,
        out_shape=(
            jax.ShapeDtypeStruct((2, BS, M), BF16),
            jax.ShapeDtypeStruct((8, BS), F32),
        ),
        in_specs=[smem, smem, smem, hbm, hbm, vmem, vmem, vmem],
        out_specs=(vmem, vmem),
        scratch_shapes=[
            pltpu.VMEM((2, 3, PP, BS, BS), BF16),
            pltpu.VMEM((WCH, PP * PP, PP * PP), BF16),
            pltpu.VMEM((PP, BS, BS), BF16),
            pltpu.VMEM((2, PP, BS, BS), BF16),
            pltpu.VMEM((2, PP, BS, BS), F32),
            pltpu.VMEM((8, BS), F32),
            pltpu.VMEM((NDEV, 8, BS), F32),
            dma((NDEV,)),
            dma((NDEV,)),
            dma((6, PP)),
        ],
        compiler_params=pltpu.CompilerParams(
            collective_id=1, has_side_effects=True, vmem_limit_bytes=VMEM_LIMIT
        ),
        name="product_lanczos",
    )(charges, lens, energy, partner, theta_m, env_in, right, ops_t)


def on_device(
    theta,
    boundary_env,
    right_env,
    site_tensors,
    site_mpo,
    bond_ops,
    block_energy,
    sector_charge,
    block_len,
    channel_charge,
):
    labels = sector_charge[0]
    lens = block_len[0]
    row_mask = jnp.arange(BS, dtype=jnp.int32)[None, :] < lens[:, None]
    theta_m = jnp.where(row_mask[:, :, None], theta[0], jnp.zeros((), BF16))
    blk = lax.axis_index("blk")
    lane = jnp.arange(BS, dtype=jnp.int32)
    row = jnp.zeros((BS,), jnp.int32)
    for k in range(2):
        row = row + jnp.where(lane == labels[k] + 1, 2 * blk + k + 1, 0)
        row = row + jnp.where(lane == 126 + k, labels[k], 0)
    lab_row = jnp.broadcast_to(row[None, :], (8, BS))
    w2 = jnp.transpose(site_mpo[0], (0, 3, 2, 4, 1))
    w2 = jnp.pad(w2, ((0, 0), (0, 0), (0, 0), (0, 0), (0, WP - WCH)))
    w2 = w2.reshape(2, PH * WCH, PH * WP)
    w2 = jnp.pad(w2, ((0, 0), (0, 80 - PH * WCH), (0, BS - PH * WP)))
    partner, env_in, env_out = exchange(theta_m, lab_row, site_tensors[0], w2, boundary_env)
    ops_t = jnp.swapaxes(bond_ops[0], 1, 2)
    lanczos, coef = product(
        channel_charge, lens, block_energy[0], partner, theta_m, env_in, right_env[0], ops_t
    )
    return env_out[None], lanczos[None], coef[0:2, 0][None, :]


def solution(mesh):
    return jax.shard_map(
        on_device,
        mesh=mesh,
        in_specs=(
            P("site", ("blk", "charge"), None, None),
            P(("blk", "charge"), None, None, None),
            P("site", ("blk", "charge"), None, None, None),
            P("site", None, ("blk", "charge"), None, None, None),
            P("site", None, None, None, None, None),
            P("site", None, None, None),
            P("site", ("blk", "charge")),
            P("site", ("blk", "charge")),
            P("site", ("blk", "charge")),
            P(),
        ),
        out_specs=(
            P("site", ("blk", "charge"), None, None, None),
            P("site", ("blk", "charge"), None, None),
            P("site", None),
        ),
        check_vma=False,
    )
```

time: 698 us -> 215 us (0.31); the launches traced: 685 us -> 215 us
  Pallas kernels: 0 us -> 198 us
  waiting for transfers between devices: 174 us -> 0 us
  matrix products: 161 us -> 0 us
  blocking collectives: 148 us -> 0 us
  loops' own time: 52.4 us -> 0 us
  local copies, waits for them, and re-layouts: 62.4 us -> 10.4 us
  other arithmetic: 56 us -> 4.36 us
  between operations: 17.4 us -> 1.98 us
  starting transfers between devices: 13.8 us -> 0 us
    pallas_call x0 -> x2, Pallas kernels: none -> 198 us  [the longest x1 157 us: exchange(): pl.pallas_call(exchange_kernel, out_shape=(jax.ShapeDtypeStruct((NBLK, 4,...]
    dot_general x85 -> x0, matrix products: 161 us -> none  [the longest x36 48.7 us: segment(): jnp.dot(left_block, source_tile, preferred_element_type=jnp.float32)]
    psum x2 -> x0, blocking collectives: 135 us -> none  [the longest x1 68.7 us: on_device(): lax.psum((jnp.sum(theta_f * product), jnp.sum(theta_f * theta_f)), ('blk'...]
    ppermute x5 -> x0, waiting for transfers between devices: 97.3 us -> none  [the longest x3 97.3 us: from_behind(): return lax.ppermute(block, axis, route)]
    all_gather x1 -> x0, waiting for transfers between devices: 77.2 us -> none  [on_device(): lax.all_gather(theta_m, 'blk', axis=0, tiled=True)]
    another operation x9 -> x0, loops' own time: 52.4 us -> none  [the longest x2 51.2 us: block_product(): lax.scan(segment, start_sum, (env_block, right_blocks, ops, charges))[0]]
    add x37 -> x1, other arithmetic: 27.2 us -> 1.3 us  [on_device(): row = row + jnp.where(lane == 126 + k, labels[k], 0)]
    dynamic_slice x36 -> x0, local copies, waits for them, and re-layouts: 23.9 us -> none  [block_product(): lax.scan(segment, start_sum, (env_block, right_blocks, ops, charges))[0]]
  transfers between devices with their start and end apart: 6 -> 0, of which waited for: 3 -> 0; matrix products, arithmetic and copies ran while one was open for 6% -> 0% of each run, Pallas kernels for 0% -> 0%
where the time goes in v1:
time: 215 us
  Pallas kernels  198 us (92%)
  local copies, waits for them, and re-layouts  10.4 us (5%)
  other arithmetic  4.36 us (2%)
    pallas_call x1, Pallas kernels, exchange(): pl.pallas_call(exchange_kernel, out_shape=(jax.ShapeDtypeStruct((NBLK, 4,...  157 us
    pallas_call x1, Pallas kernels, product(): pl.pallas_call(product_kernel, out_shape=(jax.ShapeDtypeStruct((2, BS, M)...  41.3 us
    unnamed x6, local copies, waits for them, and re-layouts  6.36 us

profile of v1, /device:TPU:97, one launch (start us, length us, event | category | flops | bytes accessed | tf_op | source)
XLA Modules:
  0.0 214.6 jit_solution(1427065338008657520)
XLA Ops:
  0.6 0.7 iota_compare_fusion
  1.4 1.3 fusion.3
  4.0 1.3 fusion.2
  5.3 0.6 broadcast_in_dim.53.lab_ref
  5.9 1.7 copy.16
  7.5 1.2 copy.17
  8.8 0.1 pad.8.clone
  8.8 0.1 reshape.54
  9.0 0.6 pad.9.w2_ref
  9.6 2.3 %bitcast_select_fusion.theta_ref = bf16[2,128,2048]{2,1,0:T(8,128)(2,1)} fusion(bf16[1,2,128,2048]{3,2,1,0:T(8,128)(2,1)} %param.10, pred[2,128]{1,0:T(4,128)(4,1)S(1)} %iota_compare_fusion), kind=kLoop, calls=%fused_computation | loop fusion | flops 524288 | bytes 2097408 | tf_op jit(solution)/shard_map/jit(_where)/select_n | solution.py:602
  11.9 156.6 %exchange_chain.1 = (bf16[16,4,128,128]{3,2,1,0:T(8,128)(2,1)}, bf16[2,18,128,128]{3,2,1,0:T(8,128)(2,1)}, bf16[2,18,128,128]{3,2,1,0:T(8,128)(2,1)}) custom-call(bf16[2,128,2048]{2,1,0:T(8,128)(2,1)} %bitcast_select_fusion.theta_ref, s32[8,128]{1,0:T(8,128)} %broadcast_in_dim.53.lab_ref, bf16[2,2,4,128,128]{4,3,2,1,0:T(8,128)(2,1)} %bitcast.20, ...), custom_call_target="tpu_custom_call" | custom-call | tf_op jit(solution)/shard_map/exchange_chain/pallas_call | solution.py:299
  168.5 41.3 %product_lanczos.1 = (bf16[2,128,2048]{2,1,0:T(8,128)(2,1)}, f32[8,128]{1,0:T(8,128)}) custom-call(s32[18]{0:T(128)} %charge_ref.1, s32[2]{0:T(128)} %bitcast.24, f32[2]{0:T(128)} %bitcast.25, bf16[16,4,128,128]{3,2,1,0:T(8,128)(2,1)} %get-tuple-element.9.partner_ref, bf16[2,128,2048]{2,1,0:T(8,128)(2,1)} %bitcast_select_fusion.theta_ref, ...), custom_call_target="tpu_custom_call" | custom-call | tf_op jit(solution)/shard_map/product_lanczos/pallas_call | solution.py:560
  209.8 1.3 slice_reduce_fusion
  211.1 0.0 copy-start
  211.1 2.5 %copy.20 = bf16[1,2,18,128,128]{4,3,2,1,0:T(8,128)(2,1)} copy(bf16[1,2,18,128,128]{4,3,2,1,0:T(8,128)(2,1)} %bitcast.17) | data formatting | bytes 2359296
  213.6 0.0 copy-done
  213.6 1.0 copy.21
Async XLA Ops:
  211.1 2.5 %copy-start = (bf16[2,128,2048]{2,1,0:T(8,128)(2,1)S(1)}, bf16[2,128,2048]{2,1,0:T(8,128)(2,1)}, u32[]{:S(2)}) copy-start(bf16[2,128,2048]{2,1,0:T(8,128)(2,1)} %get-tuple-element.11) | copy-start | bytes 3145732

commit v2 on v0

v2 whole, which is shorter than its diff:
```python
import jax
import jax.numpy as jnp
from jax import lax
from jax.experimental import pallas as pl
from jax.experimental.pallas import tpu as pltpu
from jax.sharding import PartitionSpec as P

BS = 128
PH = 4
WCH = 18
WP = 24
MS = 73
CH = 64
GRP = 6
PRE = 2
PP = 16
M = 2048
NS = 64
SEC = 4
NBLK = 16
NDEV = 32
F32 = jnp.float32
BF16 = jnp.bfloat16
MESH = pl.DeviceIdType.MESH
VMEM_LIMIT = 64 * 1024 * 1024 - 64 * 1024


def mm(a, b):
    return jnp.dot(a, b, preferred_element_type=F32)


def loop(low, high, body):
    def step(i, carry):
        body(i)
        return carry

    lax.fori_loop(low, high, step, 0)


def env_site(a_ref, w_ref, l_ref, m_ref, at_ref, out_ref):
    for t in range(PH):
        at_ref[:, t * BS : (t + 1) * BS] = a_ref[t].T
    a_cat = jnp.concatenate([a_ref[s] for s in range(PH)], axis=1)
    w2 = w_ref[:, : PH * WP]

    def chunk(ci):
        base = pl.multiple_of(ci * (CH * WP), CH * WP)
        left = mm(l_ref[pl.ds(base, CH * WP), :].astype(BF16), a_cat)
        for j in range(0, CH, 2):
            sides = []
            for e in (j, j + 1):
                rows = left[e * WP : (e + 1) * WP]
                sides.append(
                    jnp.concatenate([rows[:, s * BS : (s + 1) * BS] for s in range(PH)], axis=0)
                )
            mixed = mm(w2, jnp.concatenate(sides, axis=1).astype(BF16))
            for e in range(2):
                m_ref[pl.ds((ci * CH + j + e) * MS, PH * WCH), :] = mixed[
                    : PH * WCH, e * BS : (e + 1) * BS
                ]

    loop(0, BS // CH, chunk)

    for v in range(0, WCH, 2):
        sides = []
        for e in range(2):
            sides.append(
                jnp.concatenate(
                    [m_ref[pl.ds(t * WCH + v + e, BS, stride=MS), :] for t in range(PH)], axis=0
                )
            )
        new = mm(at_ref[...], jnp.concatenate(sides, axis=1).astype(BF16))
        for e in range(2):
            one = new[:, e * BS : (e + 1) * BS]
            out_ref[v + e] = one.astype(BF16)
            l_ref[pl.ds(v + e, BS, stride=WP), :] = one


def build_kron(ops_ref, kron):
    big = (PP * PP, PP)
    rep = (
        lax.div(lax.broadcasted_iota(jnp.int32, big, 0), PP)
        == lax.broadcasted_iota(jnp.int32, big, 1)
    ).astype(F32).astype(BF16)
    wide = (PP, PP * PP)
    rep_t = (
        lax.div(lax.broadcasted_iota(jnp.int32, wide, 1), PP)
        == lax.broadcasted_iota(jnp.int32, wide, 0)
    ).astype(F32).astype(BF16)
    full = (PP * PP, PP * PP)
    same = lax.rem(lax.broadcasted_iota(jnp.int32, full, 0), PP) == lax.rem(
        lax.broadcasted_iota(jnp.int32, full, 1), PP
    )

    def one(w):
        rows = lax.dot_general(
            rep, ops_ref[w], (((1,), (1,)), ((), ())), preferred_element_type=F32
        ).astype(BF16)
        kron[w] = jnp.where(same, mm(rows, rep_t), 0.0).astype(BF16)

    loop(0, WCH, one)


def block_product(charge_ref, kron, tiles, env_ref, right_ref, mixed, states, acc):
    def group(wi):
        for e in range(GRP):
            w = wi * GRP + e
            charge = charge_ref[w]
            c = jnp.where(charge == 0, 2, jnp.where(charge < 0, 0, 1))
            big = kron[w]
            for g in range(4):
                sides = []
                for h in range(2):
                    r0 = (g * 2 + h) * 16
                    sides.append(tiles[:, c, r0 : r0 + 16, :].reshape(PP * 16, BS))
                part = mm(big, jnp.concatenate(sides, axis=1)).astype(BF16)
                for h in range(2):
                    r0 = (g * 2 + h) * 16
                    mixed[e, :, r0 : r0 + 16, :] = part[:, h * BS : (h + 1) * BS].reshape(
                        PP, 16, BS
                    )
        for e in range(GRP):
            env = env_ref[wi * GRP + e]
            for t in range(0, PP, 2):
                part = mm(env, jnp.concatenate([mixed[e, t], mixed[e, t + 1]], axis=1))
                part = part.astype(BF16)
                states[e, t] = part[:, :BS]
                states[e, t + 1] = part[:, BS:]
        right = right_ref[pl.ds(wi * GRP, GRP)].reshape(GRP * BS, BS)
        for t in range(0, PP, 4):
            both = jnp.concatenate(
                [states[e, t : t + 4].reshape(4 * BS, BS) for e in range(GRP)], axis=1
            )
            acc[t : t + 4] += mm(both, right).reshape(4, BS, BS)

    acc[...] = jnp.zeros_like(acc)
    loop(0, WCH // GRP, group)


def sweep_kernel(
    charge_ref,
    len_ref,
    energy_ref,
    label_ref,
    theta_ref,
    tens_ref,
    w2_ref,
    benv_ref,
    right_ref,
    ops_ref,
    lanczos_ref,
    coef_ref,
    envout_ref,
    tiles_a,
    tiles_b,
    recv1,
    send2,
    lab_mine,
    lab_all,
    inv,
    lab_s,
    inv_s,
    tens,
    w2,
    left,
    mixer,
    at,
    envs,
    benv,
    right,
    kron,
    mixed,
    states,
    acc,
    mine,
    stats,
    lab_send,
    lab_recv,
    one_send,
    one_recv,
    two_send,
    two_recv,
    ten_send,
    ten_recv,
    w_send,
    w_recv,
    env_send,
    env_recv,
    stat_send,
    stat_recv,
    local,
    tile_sem,
):
    z = lax.axis_index("site")
    blk = lax.axis_index("blk")
    core = lax.axis_index("charge")
    me = blk * 2 + core
    first = lax.div(z, 3)
    other = 1 - first
    tiles = (tiles_a, tiles_b)
    order = (first, other)

    def plane(off):
        dev = lax.rem(me + off, NDEV)
        return {"blk": lax.div(dev, 2), "charge": lax.rem(dev, 2)}

    barrier = pltpu.get_barrier_semaphore()
    loop(
        1,
        NDEV,
        lambda off: pl.semaphore_signal(
            barrier, inc=1, device_id=plane(off), device_id_type=MESH
        ),
    )
    for off in range(1, SEC):
        pl.semaphore_signal(
            barrier, inc=1, device_id={"site": lax.rem(z + off, SEC)}, device_id_type=MESH
        )

    def tile_load(turn, s):
        return pltpu.make_async_copy(
            theta_ref.at[order[turn], :, pl.ds(pl.multiple_of(s * BS, BS), BS)],
            tiles[turn].at[s, 2],
            tile_sem.at[turn, s],
        )

    for turn in range(2):
        loop(0, PP, lambda s: tile_load(turn, s).start())
    loads = [
        pltpu.make_async_copy(benv_ref, benv, local.at[0]),
        pltpu.make_async_copy(tens_ref, tens.at[z], local.at[1]),
        pltpu.make_async_copy(w2_ref, w2.at[z, 0], local.at[2]),
        pltpu.make_async_copy(w2_ref, w2.at[z, 1], local.at[3]),
        pltpu.make_async_copy(right_ref, right, local.at[4]),
    ]
    for copy in loads:
        copy.start()

    lane = lax.broadcasted_iota(jnp.int32, (8, BS), 1)
    row = jnp.zeros((8, BS), jnp.int32)
    for k in range(2):
        row = row + jnp.where(lane == label_ref[0, k] + 1, 2 * blk + k + 1, 0)
        row = row + jnp.where(lane == 126 + k, label_ref[0, k], 0)
    lab_mine[...] = row
    lab_all[me] = row
    recv1[0] = jnp.zeros((BS, BS), BF16)
    rows = lax.broadcasted_iota(jnp.int32, (BS, BS), 0)

    def mask(s):
        for turn in range(2):
            tile_load(turn, s).wait()
            tile = tiles[turn][s, 2].astype(F32)
            tiles[turn][s, 2] = jnp.where(rows < len_ref[0, order[turn]], tile, 0.0).astype(BF16)

    loop(0, PP, mask)
    for turn in range(2):
        recv1[1 + 2 * blk + order[turn]] = tiles[turn][blk, 2]
    pl.semaphore_wait(barrier, NDEV - 1 + SEC - 1)

    def labels_to(off, peer):
        return pltpu.make_async_remote_copy(
            src_ref=lab_mine,
            dst_ref=lab_all.at[me],
            send_sem=lab_send.at[off],
            recv_sem=lab_recv.at[peer],
            device_id=plane(off),
            device_id_type=MESH,
        )

    def piece_to(turn, off, peer):
        dev = lax.rem(blk + off, NBLK)
        return pltpu.make_async_remote_copy(
            src_ref=tiles[turn].at[dev, 2],
            dst_ref=recv1.at[1 + 2 * blk + order[turn]],
            send_sem=one_send.at[turn, off],
            recv_sem=one_recv.at[turn, peer],
            device_id={"blk": dev},
            device_id_type=MESH,
        )

    def picked_to(turn, off, peer):
        dev = lax.rem(blk + off, NBLK)
        return pltpu.make_async_remote_copy(
            src_ref=send2.at[turn, dev],
            dst_ref=tiles[turn].at[blk, pl.ds(0, 2)],
            send_sem=two_send.at[turn, off],
            recv_sem=two_recv.at[turn, peer],
            device_id={"blk": dev, "charge": 1 - core},
            device_id_type=MESH,
        )

    def tensors_to(dst, k, sec):
        return pltpu.make_async_remote_copy(
            src_ref=tens_ref.at[:, k],
            dst_ref=tens.at[z, :, k],
            send_sem=ten_send.at[dst, k],
            recv_sem=ten_recv.at[sec, k],
            device_id={"site": dst},
            device_id_type=MESH,
        )

    def mixer_to(dst, k, sec):
        return pltpu.make_async_remote_copy(
            src_ref=w2_ref,
            dst_ref=w2.at[z, k],
            send_sem=w_send.at[dst, k],
            recv_sem=w_recv.at[sec, k],
            device_id={"site": dst},
            device_id_type=MESH,
        )

    routes = (
        (0, 1, 0), (0, 3, 1), (0, 1, 1), (0, 2, 0),
        (1, 2, 0), (1, 3, 1), (2, 3, 1), (3, 2, 0),
    )

    loop(1, NDEV, lambda off: labels_to(off, me).start())
    for src, dst, k in routes:

        @pl.when(z == src)
        def _():
            mixer_to(dst, k, src).start()
            tensors_to(dst, k, src).start()

    for turn in range(2):
        loop(1, NBLK, lambda off: piece_to(turn, off, blk).start())

    build_kron(ops_ref, kron)
    for copy in loads:
        copy.wait()
    for k in range(2):

        @pl.when((z < 2) | (z == k + 2))
        def _():
            left[k] = jnp.zeros((BS * WP, BS), F32)

            def one(v):
                left[k, pl.ds(v, BS, stride=WP), :] = benv[k, v].astype(F32)

            loop(0, WCH, one)

        @pl.when(z == 0)
        def _():
            envs[0, k] = benv[k]

    def send_picked():
        loop(1, NDEV, lambda off: labels_to(off, lax.rem(me + off, NDEV)).wait_recv())
        total = jnp.zeros((8, BS), jnp.int32)
        for i in range(NBLK):
            total = total + lab_all[2 * i + core]
        inv[...] = total
        to_s0 = pltpu.make_async_copy(lab_all, lab_s, local.at[5])
        to_s0.start()
        to_s1 = pltpu.make_async_copy(inv, inv_s, local.at[6])
        to_s1.start()
        to_s0.wait()
        to_s1.wait()
        for turn in range(2):
            loop(1, NBLK, lambda off: piece_to(turn, off, lax.rem(blk + off, NBLK)).wait_recv())
        for turn in range(2):

            def pick(dev):
                label = lab_s[2 * dev + (1 - core), 0, 126 + order[turn]]
                for gi in range(2):
                    send2[turn, dev, gi] = recv1[inv_s[0, label + 2 * gi]]

            loop(0, NBLK, pick)
            loop(0, NBLK, lambda off: picked_to(turn, off, blk).start())

    def env_to(slot, dst_slot, k, dst, which):
        return pltpu.make_async_remote_copy(
            src_ref=envs.at[slot, k],
            dst_ref=envs.at[dst_slot, k],
            send_sem=env_send.at[which],
            recv_sem=env_recv.at[which],
            device_id={"site": dst},
            device_id_type=MESH,
        )

    env_routes = ((2, 5, 1, 0, 0, 3, 0), (2, 7, 2, 1, 0, 3, 1), (3, 3, 2, 0, 1, 2, 0), (3, 5, 0, 1, 1, 2, 1))

    def site(q):
        unit, i = lax.div(q, 2), lax.rem(q, 2)
        sec = jnp.where(z < 2, lax.div(unit, 2), unit)
        k = jnp.where(z < 2, lax.rem(unit, 2), z - 2)

        @pl.when(q == PRE)
        def _():
            send_picked()

        @pl.when((i == 0) & (sec != z))
        def _():
            mixer_to(0, k, sec).wait_recv()
            tensors_to(0, k, sec).wait_recv()

        slot = jnp.where(sec == z, 1, jnp.where(sec < z, 0, 2))
        slot = jnp.where((z == 3) & (sec == 1), 2, slot)
        env_site(tens.at[sec, i, k], w2.at[sec, k, i], left.at[k], mixer, at, envs.at[slot, k])
        for src, when, slot_at, dst_slot, kk, dst, which in env_routes:

            @pl.when((z == src) & (q == when))
            def _():
                env_to(slot_at, dst_slot, kk, dst, which).start()

    loop(0, jnp.where(z == 0, 4, 8), site)

    for turn in range(2):
        k = order[turn]
        loop(0, NBLK, lambda off: picked_to(turn, off, lax.rem(blk + off, NBLK)).wait_recv())
        if turn:

            @pl.when(z >= 2)
            def _():
                env_to(0, 0, 0, 0, 0).wait_recv()

        block_product(
            charge_ref, kron, tiles[turn], envs.at[0, k], right.at[k], mixed, states, acc.at[turn]
        )

    @pl.when(z >= 2)
    def _():
        env_to(0, 0, 0, 0, 1).wait_recv()

    env_store = pltpu.make_async_copy(envs.at[1], envout_ref, local.at[7])
    env_store.start()

    zero = jnp.zeros((8, BS), F32)

    def fold(x):
        return jnp.sum(x.reshape(16, 8, BS), axis=0)

    def sums_one(t, carry):
        cor, nor = carry
        for turn in range(2):
            k = order[turn]
            th = tiles[turn][t, 2].astype(F32)
            p = jnp.where(rows < len_ref[0, k], acc[turn, t], 0.0) - energy_ref[0, k] * th
            acc[turn, t] = p
            cor = cor + fold(p * th)
            nor = nor + fold(th * th)
        return cor, nor

    cor, nor = lax.fori_loop(0, PP, sums_one, (zero, zero))

    def everywhere(x):
        return jnp.broadcast_to(
            jnp.sum(jnp.sum(x, axis=0, keepdims=True), axis=1, keepdims=True), (1, BS)
        )

    cor, nor = everywhere(cor), everywhere(nor)
    rho = jnp.where(nor > 0, cor / jnp.where(nor > 0, nor, 1.0), 0.0)

    def sums_two(t, carry):
        sq, cross = carry
        for turn in range(2):
            th = tiles[turn][t, 2].astype(F32)
            r = acc[turn, t] - rho * th
            sq = sq + fold(r * r)
            cross = cross + fold(r * th)
        return sq, cross

    sq, cross = lax.fori_loop(0, PP, sums_two, (zero, zero))
    mine[...] = jnp.concatenate(
        [cor, nor, everywhere(sq), everywhere(cross), rho, jnp.zeros((3, BS), F32)], axis=0
    )
    stats[me] = mine[...]

    def stat_to(off, peer):
        return pltpu.make_async_remote_copy(
            src_ref=mine,
            dst_ref=stats.at[me],
            send_sem=stat_send.at[off],
            recv_sem=stat_recv.at[peer],
            device_id=plane(off),
            device_id_type=MESH,
        )

    loop(1, NDEV, lambda off: stat_to(off, me).start())
    loop(1, NDEV, lambda off: labels_to(off, me).wait_send())
    for turn in range(2):
        loop(1, NBLK, lambda off: piece_to(turn, off, blk).wait_send())
        loop(0, NBLK, lambda off: picked_to(turn, off, blk).wait_send())
    for src, dst, k in routes:

        @pl.when(z == src)
        def _():
            mixer_to(dst, k, src).wait_send()
            tensors_to(dst, k, src).wait_send()

    for src, when, slot_at, dst_slot, kk, dst, which in env_routes:

        @pl.when(z == src)
        def _():
            env_to(slot_at, dst_slot, kk, dst, which).wait_send()

    loop(1, NDEV, lambda off: stat_to(off, lax.rem(me + off, NDEV)).wait_recv())

    cor_all = jnp.zeros((1, BS), F32)
    nor_all = jnp.zeros((1, BS), F32)
    for i in range(NDEV):
        cor_all = cor_all + stats[i, 0:1]
        nor_all = nor_all + stats[i, 1:2]
    ray = cor_all / nor_all
    res = jnp.zeros((1, BS), F32)
    for i in range(NDEV):
        gap = stats[i, 4:5] - ray
        res = res + (stats[i, 2:3] + gap * (2.0 * stats[i, 3:4] + gap * stats[i, 1:2]))
    mean_sq = jnp.maximum(res, 0.0) / (NS * BS * M)
    scale = 1.0 / jnp.sqrt(mean_sq + 1e-06)

    def finish(t):
        for turn in range(2):
            th = tiles[turn][t, 2].astype(F32)
            lanczos_ref[order[turn], :, pl.ds(pl.multiple_of(t * BS, BS), BS)] = (
                (acc[turn, t] - ray * th) * scale
            ).astype(BF16)

    loop(0, PP, finish)
    coef_ref[...] = jnp.concatenate(
        [ray, jnp.sqrt(mean_sq), jnp.zeros((6, BS), F32)], axis=0
    )
    loop(1, NDEV, lambda off: stat_to(off, me).wait_send())
    env_store.wait()


def sweep(charges, lens, energy, labels, theta, tensors, w2, benv, right, ops):
    hbm = pl.BlockSpec(memory_space=pl.ANY)
    vmem = pl.BlockSpec(memory_space=pltpu.VMEM)
    smem = pl.BlockSpec(memory_space=pltpu.SMEM)
    dma = pltpu.SemaphoreType.DMA
    return pl.pallas_call(
        sweep_kernel,
        out_shape=(
            jax.ShapeDtypeStruct((2, BS, M), BF16),
            jax.ShapeDtypeStruct((8, BS), F32),
            jax.ShapeDtypeStruct((2, WCH, BS, BS), BF16),
        ),
        in_specs=[smem] * 4 + [hbm] * 5 + [vmem],
        out_specs=(vmem, vmem, hbm),
        scratch_shapes=[
            pltpu.VMEM((PP, 3, BS, BS), BF16),
            pltpu.VMEM((PP, 3, BS, BS), BF16),
            pltpu.VMEM((NDEV + 1, BS, BS), BF16),
            pltpu.VMEM((2, NBLK, 2, BS, BS), BF16),
            pltpu.VMEM((8, BS), jnp.int32),
            pltpu.VMEM((NDEV, 8, BS), jnp.int32),
            pltpu.VMEM((8, BS), jnp.int32),
            pltpu.SMEM((NDEV, 8, BS), jnp.int32),
            pltpu.SMEM((8, BS), jnp.int32),
            pltpu.VMEM((SEC, 2, 2, PH, BS, BS), BF16),
            pltpu.VMEM((SEC, 2, 2, 80, BS), BF16),
            pltpu.VMEM((2, BS * WP, BS), F32),
            pltpu.VMEM((BS * MS, BS), F32),
            pltpu.VMEM((BS, PH * BS), BF16),
            pltpu.VMEM((3, 2, WCH, BS, BS), BF16),
            pltpu.VMEM((2, WCH, BS, BS), BF16),
            pltpu.VMEM((2, WCH, BS, BS), BF16),
            pltpu.VMEM((WCH, PP * PP, PP * PP), BF16),
            pltpu.VMEM((GRP, PP, BS, BS), BF16),
            pltpu.VMEM((GRP, PP, BS, BS), BF16),
            pltpu.VMEM((2, PP, BS, BS), F32),
            pltpu.VMEM((8, BS), F32),
            pltpu.VMEM((NDEV, 8, BS), F32),
            dma((NDEV,)),
            dma((NDEV,)),
            dma((2, NBLK)),
            dma((2, NBLK)),
            dma((2, NBLK)),
            dma((2, NBLK)),
            dma((SEC, 2)),
            dma((SEC, 2)),
            dma((SEC, 2)),
            dma((SEC, 2)),
            dma((2,)),
            dma((2,)),
            dma((NDEV,)),
            dma((NDEV,)),
            dma((8,)),
            dma((2, PP)),
        ],
        compiler_params=pltpu.CompilerParams(
            collective_id=0, has_side_effects=True, vmem_limit_bytes=VMEM_LIMIT
        ),
        name="sweep",
    )(charges, lens, energy, labels, theta, tensors, w2, benv, right, ops)


def on_device(
    theta,
    boundary_env,
    right_env,
    site_tensors,
    site_mpo,
    bond_ops,
    block_energy,
    sector_charge,
    block_len,
    channel_charge,
):
    w2 = jnp.transpose(site_mpo[0], (0, 3, 2, 4, 1))
    w2 = jnp.pad(w2, ((0, 0), (0, 0), (0, 0), (0, 0), (0, WP - WCH)))
    w2 = w2.reshape(2, PH * WCH, PH * WP)
    w2 = jnp.pad(w2, ((0, 0), (0, 80 - PH * WCH), (0, BS - PH * WP)))
    lanczos, coef, env_out = sweep(
        channel_charge,
        block_len,
        block_energy,
        sector_charge,
        theta[0],
        site_tensors[0],
        w2,
        boundary_env,
        right_env[0],
        bond_ops[0],
    )
    return env_out[None], lanczos[None], coef[0:2, 0][None, :]


def solution(mesh):
    return jax.shard_map(
        on_device,
        mesh=mesh,
        in_specs=(
            P("site", ("blk", "charge"), None, None),
            P(("blk", "charge"), None, None, None),
            P("site", ("blk", "charge"), None, None, None),
            P("site", None, ("blk", "charge"), None, None, None),
            P("site", None, None, None, None, None),
            P("site", None, None, None),
            P("site", ("blk", "charge")),
            P("site", ("blk", "charge")),
            P("site", ("blk", "charge")),
            P(),
        ),
        out_specs=(
            P("site", ("blk", "charge"), None, None, None),
            P("site", ("blk", "charge"), None, None),
            P("site", None),
        ),
        check_vma=False,
    )
```

time: 698 us -> 97.4 us (0.14)
  the two profiles are of different devices: /device:TPU:97 before, /device:TPU:65 now
where the time goes in v2:
time: 97.4 us; the launch traced here: 97.1 us
  Pallas kernels  87.9 us (90%)
  local copies, waits for them, and re-layouts  8.49 us (9%)
    pallas_call x1, Pallas kernels, sweep(): pl.pallas_call(sweep_kernel, out_shape=(jax.ShapeDtypeStruct((2, BS, M),...  87.9 us
    unnamed x6, local copies, waits for them, and re-layouts  6.35 us

profile of v2, /device:TPU:65, one launch (start us, length us, event | category | flops | bytes accessed | tf_op | source)
XLA Modules:
  0.0 97.1 jit_solution(15096137480299683982)
XLA Ops:
  0.6 1.6 %copy.16 = bf16[1,18,16,16]{3,2,1,0:T(8,128)(2,1)} copy(bf16[1,18,16,16]{1,3,2,0:T(8,128)(2,1)} %param.15) | data formatting | bytes 18432 | tf_op args[5]
  2.3 1.2 %copy.17 = bf16[2,4,18,4,18]{4,3,2,1,0:T(4,128)(2,1)S(1)} copy(bf16[2,4,18,4,18]{2,3,1,4,0:T(4,128)(2,1)} %bitcast.16) | data formatting | bytes 41472
  3.5 0.1 pad.8.clone
  3.6 0.1 reshape.9
  3.7 0.6 pad.9.w2_ref
  4.4 87.9 %sweep.1 = (bf16[2,128,2048]{2,1,0:T(8,128)(2,1)}, f32[8,128]{1,0:T(8,128)}, bf16[2,18,128,128]{3,2,1,0:T(8,128)(2,1)}) custom-call(s32[18]{0:T(128)} %charge_ref.1, s32[1,2]{1,0:T(1,128)} %len_ref.1, f32[1,2]{1,0:T(1,128)} %energy_ref.1, s32[1,2]{1,0:T(1,128)} %label_ref.1, bf16[2,128,2048]{2,1,0:T(8,128)(2,1)} %bitcast.12, ...), custom_call_target="tpu_custom_call" | custom-call | tf_op jit(solution)/shard_map/sweep/pallas_call | solution.py:531
  92.3 1.3 %slice_reduce_fusion = f32[2]{0:T(128)} fusion(f32[8,128]{1,0:T(8,128)} %get-tuple-element.8), kind=kLoop, calls=%fused_computation | loop fusion | bytes 16 | tf_op jit(solution)/shard_map/slice | solution.py:616
  93.6 0.0 copy-start
  93.6 2.5 %copy.20 = bf16[1,2,18,128,128]{4,3,2,1,0:T(8,128)(2,1)} copy(bf16[1,2,18,128,128]{4,3,2,1,0:T(8,128)(2,1)} %bitcast.11) | data formatting | bytes 2359296
  96.1 0.0 copy-done
  96.1 1.0 copy.21
Async XLA Ops:
  93.6 2.5 %copy-start = (bf16[2,128,2048]{2,1,0:T(8,128)(2,1)S(1)}, bf16[2,128,2048]{2,1,0:T(8,128)(2,1)}, u32[]{:S(2)}) copy-start(bf16[2,128,2048]{2,1,0:T(8,128)(2,1)} %get-tuple-element.7) | copy-start | bytes 3145732

commit v3 on v2

--- a/solution.py
+++ b/solution.py
@@ -12,13 +12,18 @@
 MS = 73
 CH = 64
 GRP = 6
-PRE = 2
+PRE = 0
 PP = 16
 M = 2048
 NS = 64
 SEC = 4
 NBLK = 16
 NDEV = 32
+SIDE = 4
+STEPS = (
+    (1, 1), (3, 3), (2, 2), (1, 3), (3, 1), (2, 0), (0, 2), (1, 2),
+    (3, 2), (2, 1), (2, 3), (1, 0), (3, 0), (0, 1), (0, 3),
+)
 F32 = jnp.float32
 BF16 = jnp.bfloat16
 MESH = pl.DeviceIdType.MESH
@@ -200,6 +205,9 @@
     tiles = (tiles_a, tiles_b)
     order = (first, other)
 
+    def ahead(dx, dy):
+        return lax.rem(lax.div(blk, SIDE) + dx, SIDE) * SIDE + lax.rem(lax.rem(blk, SIDE) + dy, SIDE)
+
     def plane(off):
         dev = lax.rem(me + off, NDEV)
         return {"blk": lax.div(dev, 2), "charge": lax.rem(dev, 2)}
@@ -267,23 +275,21 @@
             device_id_type=MESH,
         )
 
-    def piece_to(turn, off, peer):
-        dev = lax.rem(blk + off, NBLK)
+    def piece_to(turn, step, dev, peer):
         return pltpu.make_async_remote_copy(
             src_ref=tiles[turn].at[dev, 2],
             dst_ref=recv1.at[1 + 2 * blk + order[turn]],
-            send_sem=one_send.at[turn, off],
+            send_sem=one_send.at[turn, step],
             recv_sem=one_recv.at[turn, peer],
             device_id={"blk": dev},
             device_id_type=MESH,
         )
 
-    def picked_to(turn, off, peer):
-        dev = lax.rem(blk + off, NBLK)
+    def picked_to(turn, step, dev, peer):
         return pltpu.make_async_remote_copy(
             src_ref=send2.at[turn, dev],
             dst_ref=tiles[turn].at[blk, pl.ds(0, 2)],
-            send_sem=two_send.at[turn, off],
+            send_sem=two_send.at[turn, step],
             recv_sem=two_recv.at[turn, peer],
             device_id={"blk": dev, "charge": 1 - core},
             device_id_type=MESH,
@@ -310,8 +316,8 @@
         )
 
     routes = (
-        (0, 1, 0), (0, 3, 1), (0, 1, 1), (0, 2, 0),
-        (1, 2, 0), (1, 3, 1), (2, 3, 1), (3, 2, 0),
+        (0, 3, 1), (0, 2, 0), (0, 1, 0), (0, 1, 1),
+        (1, 3, 1), (1, 2, 0), (2, 3, 1),
     )
 
     loop(1, NDEV, lambda off: labels_to(off, me).start())
@@ -323,21 +329,26 @@
             tensors_to(dst, k, src).start()
 
     for turn in range(2):
-        loop(1, NBLK, lambda off: piece_to(turn, off, blk).start())
+        for step, (dx, dy) in enumerate(STEPS):
+            piece_to(turn, step, ahead(dx, dy), blk).start()
 
     build_kron(ops_ref, kron)
     for copy in loads:
         copy.wait()
+
+    def load_left(k, env_ref):
+        left[k] = jnp.zeros((BS * WP, BS), F32)
+
+        def one(v):
+            left[k, pl.ds(v, BS, stride=WP), :] = env_ref[v].astype(F32)
+
+        loop(0, WCH, one)
+
     for k in range(2):
 
         @pl.when((z < 2) | (z == k + 2))
         def _():
-            left[k] = jnp.zeros((BS * WP, BS), F32)
-
-            def one(v):
-                left[k, pl.ds(v, BS, stride=WP), :] = benv[k, v].astype(F32)
-
-            loop(0, WCH, one)
+            load_left(k, benv.at[k])
 
         @pl.when(z == 0)
         def _():
@@ -356,7 +367,7 @@
         to_s0.wait()
         to_s1.wait()
         for turn in range(2):
-            loop(1, NBLK, lambda off: piece_to(turn, off, lax.rem(blk + off, NBLK)).wait_recv())
+            loop(1, NBLK, lambda i: piece_to(turn, 0, 0, lax.rem(blk + i, NBLK)).wait_recv())
         for turn in range(2):
 
             def pick(dev):
@@ -365,19 +376,20 @@
                     send2[turn, dev, gi] = recv1[inv_s[0, label + 2 * gi]]
 
             loop(0, NBLK, pick)
-            loop(0, NBLK, lambda off: picked_to(turn, off, blk).start())
-
-    def env_to(slot, dst_slot, k, dst, which):
+            for step, (dx, dy) in enumerate(((0, 0),) + STEPS):
+                picked_to(turn, step, ahead(dx, dy), blk).start()
+
+    def env_to(slot, k, dst):
         return pltpu.make_async_remote_copy(
             src_ref=envs.at[slot, k],
-            dst_ref=envs.at[dst_slot, k],
-            send_sem=env_send.at[which],
-            recv_sem=env_recv.at[which],
+            dst_ref=envs.at[0, k],
+            send_sem=env_send,
+            recv_sem=env_recv,
             device_id={"site": dst},
             device_id_type=MESH,
         )
 
-    env_routes = ((2, 5, 1, 0, 0, 3, 0), (2, 7, 2, 1, 0, 3, 1), (3, 3, 2, 0, 1, 2, 0), (3, 5, 0, 1, 1, 2, 1))
+    env_routes = ((2, 5, 1, 0, 3), (3, 3, 2, 1, 2))
 
     def site(q):
         unit, i = lax.div(q, 2), lax.rem(q, 2)
@@ -393,36 +405,38 @@
             mixer_to(0, k, sec).wait_recv()
             tensors_to(0, k, sec).wait_recv()
 
-        slot = jnp.where(sec == z, 1, jnp.where(sec < z, 0, 2))
+        slot = jnp.where(sec == z, 1, 0)
         slot = jnp.where((z == 3) & (sec == 1), 2, slot)
         env_site(tens.at[sec, i, k], w2.at[sec, k, i], left.at[k], mixer, at, envs.at[slot, k])
-        for src, when, slot_at, dst_slot, kk, dst, which in env_routes:
+        for src, when, slot_at, kk, dst in env_routes:
 
             @pl.when((z == src) & (q == when))
             def _():
-                env_to(slot_at, dst_slot, kk, dst, which).start()
-
-    loop(0, jnp.where(z == 0, 4, 8), site)
+                env_to(slot_at, kk, dst).start()
+
+    loop(0, jnp.where(z == 0, 4, jnp.where(z == 2, 6, 8)), site)
+
+    def late_sites():
+        env_to(0, 0, 0).wait_recv()
+        load_left(other, envs.at[0, other])
+
+        def late(i):
+            env_site(
+                tens.at[z, i, other], w2.at[z, other, i], left.at[other], mixer, at, envs.at[1, other]
+            )
+
+        loop(0, 2, late)
 
     for turn in range(2):
         k = order[turn]
-        loop(0, NBLK, lambda off: picked_to(turn, off, lax.rem(blk + off, NBLK)).wait_recv())
         if turn:
-
-            @pl.when(z >= 2)
-            def _():
-                env_to(0, 0, 0, 0, 0).wait_recv()
-
+            pl.when(z >= 2)(late_sites)
+            env_store = pltpu.make_async_copy(envs.at[1], envout_ref, local.at[7])
+            env_store.start()
+        loop(0, NBLK, lambda i: picked_to(turn, 0, 0, lax.rem(blk + i, NBLK)).wait_recv())
         block_product(
             charge_ref, kron, tiles[turn], envs.at[0, k], right.at[k], mixed, states, acc.at[turn]
         )
-
-    @pl.when(z >= 2)
-    def _():
-        env_to(0, 0, 0, 0, 1).wait_recv()
-
-    env_store = pltpu.make_async_copy(envs.at[1], envout_ref, local.at[7])
-    env_store.start()
 
     zero = jnp.zeros((8, BS), F32)
 
@@ -478,8 +492,8 @@
     loop(1, NDEV, lambda off: stat_to(off, me).start())
     loop(1, NDEV, lambda off: labels_to(off, me).wait_send())
     for turn in range(2):
-        loop(1, NBLK, lambda off: piece_to(turn, off, blk).wait_send())
-        loop(0, NBLK, lambda off: picked_to(turn, off, blk).wait_send())
+        loop(0, NBLK - 1, lambda step: piece_to(turn, step, 0, blk).wait_send())
+        loop(0, NBLK, lambda step: picked_to(turn, step, 0, blk).wait_send())
     for src, dst, k in routes:
 
         @pl.when(z == src)
@@ -487,11 +501,11 @@
             mixer_to(dst, k, src).wait_send()
             tensors_to(dst, k, src).wait_send()
 
-    for src, when, slot_at, dst_slot, kk, dst, which in env_routes:
+    for src, when, slot_at, kk, dst in env_routes:
 
         @pl.when(z == src)
         def _():
-            env_to(slot_at, dst_slot, kk, dst, which).wait_send()
+            env_to(slot_at, kk, dst).wait_send()
 
     loop(1, NDEV, lambda off: stat_to(off, lax.rem(me + off, NDEV)).wait_recv())
 
@@ -516,9 +530,8 @@
             ).astype(BF16)
 
     loop(0, PP, finish)
-    coef_ref[...] = jnp.concatenate(
-        [ray, jnp.sqrt(mean_sq), jnp.zeros((6, BS), F32)], axis=0
-    )
+    coef_ref[0, 0] = ray[0, 0]
+    coef_ref[0, 1] = jnp.sqrt(mean_sq)[0, 0]
     loop(1, NDEV, lambda off: stat_to(off, me).wait_send())
     env_store.wait()
 
@@ -532,11 +545,11 @@
         sweep_kernel,
         out_shape=(
             jax.ShapeDtypeStruct((2, BS, M), BF16),
-            jax.ShapeDtypeStruct((8, BS), F32),
+            jax.ShapeDtypeStruct((1, 2), F32),
             jax.ShapeDtypeStruct((2, WCH, BS, BS), BF16),
         ),
         in_specs=[smem] * 4 + [hbm] * 5 + [vmem],
-        out_specs=(vmem, vmem, hbm),
+        out_specs=(vmem, smem, hbm),
         scratch_shapes=[
             pltpu.VMEM((PP, 3, BS, BS), BF16),
             pltpu.VMEM((PP, 3, BS, BS), BF16),
@@ -571,8 +584,8 @@
             dma((SEC, 2)),
             dma((SEC, 2)),
             dma((SEC, 2)),
-            dma((2,)),
-            dma((2,)),
+            dma,
+            dma,
             dma((NDEV,)),
             dma((NDEV,)),
             dma((8,)),
@@ -613,7 +626,7 @@
         right_env[0],
         bond_ops[0],
     )
-    return env_out[None], lanczos[None], coef[0:2, 0][None, :]
+    return env_out[None], lanczos[None], coef
 
 
 def solution(mesh):

time: 97.4 us -> 85.3 us (0.88)
  the two profiles are of different devices: /device:TPU:65 before, /device:TPU:97 now
where the time goes in v3:
time: 85.3 us; the launch traced here: 85.1 us
  Pallas kernels  76.7 us (90%)
  local copies, waits for them, and re-layouts  7.7 us (9%)
    pallas_call x1, Pallas kernels, sweep(): pl.pallas_call(sweep_kernel, out_shape=(jax.ShapeDtypeStruct((2, BS, M),...  76.7 us
    unnamed x9, local copies, waits for them, and re-layouts  6.86 us

profile of v3, /device:TPU:97, one launch (start us, length us, event | category | flops | bytes accessed | tf_op | source)
XLA Modules:
  0.0 85.1 jit_solution(13040993168309067203)
XLA Ops:
  0.6 1.6 %copy.14 = bf16[1,18,16,16]{3,2,1,0:T(8,128)(2,1)} copy(bf16[1,18,16,16]{1,3,2,0:T(8,128)(2,1)} %param.15) | data formatting | bytes 18432 | tf_op args[5]
  2.3 1.2 %copy.15 = bf16[2,4,18,4,18]{4,3,2,1,0:T(4,128)(2,1)S(1)} copy(bf16[2,4,18,4,18]{2,3,1,4,0:T(4,128)(2,1)} %bitcast.15) | data formatting | bytes 41472
  3.5 0.1 pad.8.clone
  3.6 0.1 reshape.9
  3.7 0.6 pad.9.w2_ref
  4.4 76.7 %sweep.1 = (bf16[2,128,2048]{2,1,0:T(8,128)(2,1)}, f32[1,2]{1,0:T(1,128)}, bf16[2,18,128,128]{3,2,1,0:T(8,128)(2,1)}) custom-call(s32[18]{0:T(128)} %charge_ref.1, s32[1,2]{1,0:T(1,128)} %len_ref.1, f32[1,2]{1,0:T(1,128)} %energy_ref.1, s32[1,2]{1,0:T(1,128)} %label_ref.1, bf16[2,128,2048]{2,1,0:T(8,128)(2,1)} %bitcast.11, ...), custom_call_target="tpu_custom_call" | custom-call | tf_op jit(solution)/shard_map/sweep/pallas_call | solution.py:544
  81.1 0.0 copy-start
  81.1 2.5 %copy.19 = bf16[1,2,18,128,128]{4,3,2,1,0:T(8,128)(2,1)} copy(bf16[1,2,18,128,128]{4,3,2,1,0:T(8,128)(2,1)} %bitcast.10) | data formatting | bytes 2359296
  83.6 0.0 copy-done
  83.6 0.0 copy-start.1
  83.6 1.0 %copy.20 = bf16[1,2,128,2048]{3,2,1,0:T(8,128)(2,1)} copy(bf16[1,2,128,2048]{3,2,1,0:T(8,128)(2,1)S(1)} %bitcast.12) | data formatting | bytes 2097152
  84.6 0.0 copy-done.1
  84.6 0.5 copy.21
Async XLA Ops:
  81.1 2.5 %copy-start = (bf16[2,128,2048]{2,1,0:T(8,128)(2,1)S(1)}, bf16[2,128,2048]{2,1,0:T(8,128)(2,1)}, u32[]{:S(2)}) copy-start(bf16[2,128,2048]{2,1,0:T(8,128)(2,1)} %get-tuple-element.7) | copy-start | bytes 3145732
  83.6 1.0 %copy-start.1 = (f32[1,2]{1,0:T(1,128)S(1)}, f32[1,2]{1,0:T(1,128)}, u32[]{:S(2)}) copy-start(f32[1,2]{1,0:T(1,128)} %get-tuple-element.14) | copy-start | bytes 28

commit v4 on v3

--- a/solution.py
+++ b/solution.py
@@ -10,7 +10,7 @@
 WCH = 18
 WP = 24
 MS = 73
-CH = 64
+CH = 128
 GRP = 6
 PRE = 0
 PP = 16
@@ -27,7 +27,7 @@
 F32 = jnp.float32
 BF16 = jnp.bfloat16
 MESH = pl.DeviceIdType.MESH
-VMEM_LIMIT = 64 * 1024 * 1024 - 64 * 1024
+VMEM_LIMIT = 64 * 1024 * 1024 - 2400 * 1024
 
 
 def mm(a, b):
@@ -162,9 +162,8 @@
     send2,
     lab_mine,
     lab_all,
-    inv,
-    lab_s,
-    inv_s,
+    table,
+    table_s,
     tens,
     w2,
     left,
@@ -173,6 +172,7 @@
     envs,
     benv,
     right,
+    ops,
     kron,
     mixed,
     states,
@@ -208,6 +208,9 @@
     def ahead(dx, dy):
         return lax.rem(lax.div(blk, SIDE) + dx, SIDE) * SIDE + lax.rem(lax.rem(blk, SIDE) + dy, SIDE)
 
+    def arrived(ref, sem):
+        pltpu.make_async_copy(ref, ref, sem).wait()
+
     def plane(off):
         dev = lax.rem(me + off, NDEV)
         return {"blk": lax.div(dev, 2), "charge": lax.rem(dev, 2)}
@@ -229,7 +232,7 @@
         return pltpu.make_async_copy(
             theta_ref.at[order[turn], :, pl.ds(pl.multiple_of(s * BS, BS), BS)],
             tiles[turn].at[s, 2],
-            tile_sem.at[turn, s],
+            tile_sem.at[turn],
         )
 
     for turn in range(2):
@@ -240,15 +243,18 @@
         pltpu.make_async_copy(w2_ref, w2.at[z, 0], local.at[2]),
         pltpu.make_async_copy(w2_ref, w2.at[z, 1], local.at[3]),
         pltpu.make_async_copy(right_ref, right, local.at[4]),
+        pltpu.make_async_copy(ops_ref, ops, local.at[6]),
     ]
     for copy in loads:
         copy.start()
 
     lane = lax.broadcasted_iota(jnp.int32, (8, BS), 1)
+    line = lax.broadcasted_iota(jnp.int32, (8, BS), 0)
     row = jnp.zeros((8, BS), jnp.int32)
     for k in range(2):
-        row = row + jnp.where(lane == label_ref[0, k] + 1, 2 * blk + k + 1, 0)
-        row = row + jnp.where(lane == 126 + k, label_ref[0, k], 0)
+        here = (line == core) & (lane == label_ref[0, k] + 1)
+        row = row + jnp.where(here, 2 * blk + k + 1, 0)
+        row = row + jnp.where((line == 2) & (lane == 2 * me + k), label_ref[0, k], 0)
     lab_mine[...] = row
     lab_all[me] = row
     recv1[0] = jnp.zeros((BS, BS), BF16)
@@ -256,41 +262,42 @@
 
     def mask(s):
         for turn in range(2):
-            tile_load(turn, s).wait()
             tile = tiles[turn][s, 2].astype(F32)
             tiles[turn][s, 2] = jnp.where(rows < len_ref[0, order[turn]], tile, 0.0).astype(BF16)
 
+    for turn in range(2):
+        arrived(tiles[turn].at[:, 2], tile_sem.at[turn])
     loop(0, PP, mask)
     for turn in range(2):
         recv1[1 + 2 * blk + order[turn]] = tiles[turn][blk, 2]
     pl.semaphore_wait(barrier, NDEV - 1 + SEC - 1)
 
-    def labels_to(off, peer):
+    def labels_to(off):
         return pltpu.make_async_remote_copy(
             src_ref=lab_mine,
             dst_ref=lab_all.at[me],
-            send_sem=lab_send.at[off],
-            recv_sem=lab_recv.at[peer],
+            send_sem=lab_send,
+            recv_sem=lab_recv,
             device_id=plane(off),
             device_id_type=MESH,
         )
 
-    def piece_to(turn, step, dev, peer):
+    def piece_to(turn, dev):
         return pltpu.make_async_remote_copy(
             src_ref=tiles[turn].at[dev, 2],
             dst_ref=recv1.at[1 + 2 * blk + order[turn]],
-            send_sem=one_send.at[turn, step],
-            recv_sem=one_recv.at[turn, peer],
+            send_sem=one_send,
+            recv_sem=one_recv,
             device_id={"blk": dev},
             device_id_type=MESH,
         )
 
-    def picked_to(turn, step, dev, peer):
+    def picked_to(turn, dev):
         return pltpu.make_async_remote_copy(
             src_ref=send2.at[turn, dev],
             dst_ref=tiles[turn].at[blk, pl.ds(0, 2)],
-            send_sem=two_send.at[turn, step],
-            recv_sem=two_recv.at[turn, peer],
+            send_sem=two_send.at[turn],
+            recv_sem=two_recv.at[turn],
             device_id={"blk": dev, "charge": 1 - core},
             device_id_type=MESH,
         )
@@ -320,7 +327,7 @@
         (1, 3, 1), (1, 2, 0), (2, 3, 1),
     )
 
-    loop(1, NDEV, lambda off: labels_to(off, me).start())
+    loop(1, NDEV, lambda off: labels_to(off).start())
     for src, dst, k in routes:
 
         @pl.when(z == src)
@@ -329,12 +336,12 @@
             tensors_to(dst, k, src).start()
 
     for turn in range(2):
-        for step, (dx, dy) in enumerate(STEPS):
-            piece_to(turn, step, ahead(dx, dy), blk).start()
-
-    build_kron(ops_ref, kron)
+        for dx, dy in STEPS:
+            piece_to(turn, ahead(dx, dy)).start()
+
     for copy in loads:
         copy.wait()
+    build_kron(ops, kron)
 
     def load_left(k, env_ref):
         left[k] = jnp.zeros((BS * WP, BS), F32)
@@ -355,29 +362,25 @@
             envs[0, k] = benv[k]
 
     def send_picked():
-        loop(1, NDEV, lambda off: labels_to(off, lax.rem(me + off, NDEV)).wait_recv())
+        arrived(lab_all.at[pl.ds(0, NDEV - 1)], lab_recv)
         total = jnp.zeros((8, BS), jnp.int32)
-        for i in range(NBLK):
-            total = total + lab_all[2 * i + core]
-        inv[...] = total
-        to_s0 = pltpu.make_async_copy(lab_all, lab_s, local.at[5])
-        to_s0.start()
-        to_s1 = pltpu.make_async_copy(inv, inv_s, local.at[6])
-        to_s1.start()
-        to_s0.wait()
-        to_s1.wait()
+        for i in range(NDEV):
+            total = total + lab_all[i]
+        table[...] = total
+        to_scalar = pltpu.make_async_copy(table, table_s, local.at[5])
+        to_scalar.start()
+        to_scalar.wait()
+        arrived(recv1.at[pl.ds(0, 2 * NBLK - 2)], one_recv)
         for turn in range(2):
-            loop(1, NBLK, lambda i: piece_to(turn, 0, 0, lax.rem(blk + i, NBLK)).wait_recv())
-        for turn in range(2):
 
             def pick(dev):
-                label = lab_s[2 * dev + (1 - core), 0, 126 + order[turn]]
+                label = table_s[2, 4 * dev + 2 * (1 - core) + order[turn]]
                 for gi in range(2):
-                    send2[turn, dev, gi] = recv1[inv_s[0, label + 2 * gi]]
+                    send2[turn, dev, gi] = recv1[table_s[core, label + 2 * gi]]
 
             loop(0, NBLK, pick)
-            for step, (dx, dy) in enumerate(((0, 0),) + STEPS):
-                picked_to(turn, step, ahead(dx, dy), blk).start()
+            for dx, dy in STEPS + ((0, 0),):
+                picked_to(turn, ahead(dx, dy)).start()
 
     def env_to(slot, k, dst):
         return pltpu.make_async_remote_copy(
@@ -427,73 +430,71 @@
 
         loop(0, 2, late)
 
+    zero = jnp.zeros((8, BS), F32)
+
+    def fold(x):
+        return jnp.sum(x.reshape(16, 8, BS), axis=0)
+
+    def everywhere(x):
+        return jnp.broadcast_to(
+            jnp.sum(jnp.sum(x, axis=0, keepdims=True), axis=1, keepdims=True), (1, BS)
+        )
+
+    def block_sums(turn):
+        length, energy = len_ref[0, order[turn]], energy_ref[0, order[turn]]
+
+        def sums_one(t, carry):
+            cor, nor = carry
+            th = tiles[turn][t, 2].astype(F32)
+            p = jnp.where(rows < length, acc[turn, t], 0.0) - energy * th
+            acc[turn, t] = p
+            return cor + fold(p * th), nor + fold(th * th)
+
+        cor, nor = lax.fori_loop(0, PP, sums_one, (zero, zero))
+        cor, nor = everywhere(cor), everywhere(nor)
+        rho = jnp.where(nor > 0, cor / jnp.where(nor > 0, nor, 1.0), 0.0)
+
+        def sums_two(t, carry):
+            sq, cross = carry
+            th = tiles[turn][t, 2].astype(F32)
+            r = acc[turn, t] - rho * th
+            return sq + fold(r * r), cross + fold(r * th)
+
+        sq, cross = lax.fori_loop(0, PP, sums_two, (zero, zero))
+        mine[8 * turn : 8 * turn + 8] = jnp.concatenate(
+            [cor, nor, everywhere(sq), everywhere(cross), rho, jnp.zeros((3, BS), F32)], axis=0
+        )
+
     for turn in range(2):
         k = order[turn]
         if turn:
             pl.when(z >= 2)(late_sites)
             env_store = pltpu.make_async_copy(envs.at[1], envout_ref, local.at[7])
             env_store.start()
-        loop(0, NBLK, lambda i: picked_to(turn, 0, 0, lax.rem(blk + i, NBLK)).wait_recv())
+        arrived(tiles[turn].at[:, pl.ds(0, 2)], two_recv.at[turn])
         block_product(
             charge_ref, kron, tiles[turn], envs.at[0, k], right.at[k], mixed, states, acc.at[turn]
         )
-
-    zero = jnp.zeros((8, BS), F32)
-
-    def fold(x):
-        return jnp.sum(x.reshape(16, 8, BS), axis=0)
-
-    def sums_one(t, carry):
-        cor, nor = carry
-        for turn in range(2):
-            k = order[turn]
-            th = tiles[turn][t, 2].astype(F32)
-            p = jnp.where(rows < len_ref[0, k], acc[turn, t], 0.0) - energy_ref[0, k] * th
-            acc[turn, t] = p
-            cor = cor + fold(p * th)
-            nor = nor + fold(th * th)
-        return cor, nor
-
-    cor, nor = lax.fori_loop(0, PP, sums_one, (zero, zero))
-
-    def everywhere(x):
-        return jnp.broadcast_to(
-            jnp.sum(jnp.sum(x, axis=0, keepdims=True), axis=1, keepdims=True), (1, BS)
-        )
-
-    cor, nor = everywhere(cor), everywhere(nor)
-    rho = jnp.where(nor > 0, cor / jnp.where(nor > 0, nor, 1.0), 0.0)
-
-    def sums_two(t, carry):
-        sq, cross = carry
-        for turn in range(2):
-            th = tiles[turn][t, 2].astype(F32)
-            r = acc[turn, t] - rho * th
-            sq = sq + fold(r * r)
-            cross = cross + fold(r * th)
-        return sq, cross
-
-    sq, cross = lax.fori_loop(0, PP, sums_two, (zero, zero))
-    mine[...] = jnp.concatenate(
-        [cor, nor, everywhere(sq), everywhere(cross), rho, jnp.zeros((3, BS), F32)], axis=0
-    )
+        block_sums(turn)
+
+
     stats[me] = mine[...]
 
-    def stat_to(off, peer):
+    def stat_to(off):
         return pltpu.make_async_remote_copy(
             src_ref=mine,
             dst_ref=stats.at[me],
-            send_sem=stat_send.at[off],
-            recv_sem=stat_recv.at[peer],
+            send_sem=stat_send,
+            recv_sem=stat_recv,
             device_id=plane(off),
             device_id_type=MESH,
         )
 
-    loop(1, NDEV, lambda off: stat_to(off, me).start())
-    loop(1, NDEV, lambda off: labels_to(off, me).wait_send())
+    loop(1, NDEV, lambda off: stat_to(off).start())
+    arrived(lab_all.at[pl.ds(0, NDEV - 1)], lab_send)
+    arrived(recv1.at[pl.ds(0, 2 * NBLK - 2)], one_send)
     for turn in range(2):
-        loop(0, NBLK - 1, lambda step: piece_to(turn, step, 0, blk).wait_send())
-        loop(0, NBLK, lambda step: picked_to(turn, step, 0, blk).wait_send())
+        arrived(send2.at[turn], two_send.at[turn])
     for src, dst, k in routes:
 
         @pl.when(z == src)
@@ -507,18 +508,23 @@
         def _():
             env_to(slot_at, kk, dst).wait_send()
 
-    loop(1, NDEV, lambda off: stat_to(off, lax.rem(me + off, NDEV)).wait_recv())
+    arrived(stats.at[pl.ds(0, NDEV - 1)], stat_recv)
 
     cor_all = jnp.zeros((1, BS), F32)
     nor_all = jnp.zeros((1, BS), F32)
     for i in range(NDEV):
-        cor_all = cor_all + stats[i, 0:1]
-        nor_all = nor_all + stats[i, 1:2]
+        for at_row in (0, 8):
+            cor_all = cor_all + stats[i, at_row : at_row + 1]
+            nor_all = nor_all + stats[i, at_row + 1 : at_row + 2]
     ray = cor_all / nor_all
     res = jnp.zeros((1, BS), F32)
     for i in range(NDEV):
-        gap = stats[i, 4:5] - ray
-        res = res + (stats[i, 2:3] + gap * (2.0 * stats[i, 3:4] + gap * stats[i, 1:2]))
+        for at_row in (0, 8):
+            nor, sq, cross, rho = (
+                stats[i, at_row + j : at_row + j + 1] for j in (1, 2, 3, 4)
+            )
+            gap = rho - ray
+            res = res + (sq + gap * (2.0 * cross + gap * nor))
     mean_sq = jnp.maximum(res, 0.0) / (NS * BS * M)
     scale = 1.0 / jnp.sqrt(mean_sq + 1e-06)
 
@@ -532,24 +538,24 @@
     loop(0, PP, finish)
     coef_ref[0, 0] = ray[0, 0]
     coef_ref[0, 1] = jnp.sqrt(mean_sq)[0, 0]
-    loop(1, NDEV, lambda off: stat_to(off, me).wait_send())
+    arrived(stats.at[pl.ds(0, NDEV - 1)], stat_send)
     env_store.wait()
 
 
 def sweep(charges, lens, energy, labels, theta, tensors, w2, benv, right, ops):
-    hbm = pl.BlockSpec(memory_space=pl.ANY)
+    hbm = pl.BlockSpec(memory_space=pltpu.HBM)
     vmem = pl.BlockSpec(memory_space=pltpu.VMEM)
     smem = pl.BlockSpec(memory_space=pltpu.SMEM)
     dma = pltpu.SemaphoreType.DMA
     return pl.pallas_call(
         sweep_kernel,
         out_shape=(
-            jax.ShapeDtypeStruct((2, BS, M), BF16),
+            pltpu.VMEM((2, BS, M), BF16),
             jax.ShapeDtypeStruct((1, 2), F32),
-            jax.ShapeDtypeStruct((2, WCH, BS, BS), BF16),
+            pltpu.VMEM((2, WCH, BS, BS), BF16),
         ),
-        in_specs=[smem] * 4 + [hbm] * 5 + [vmem],
-        out_specs=(vmem, smem, hbm),
+        in_specs=[smem] * 4 + [hbm] * 6,
+        out_specs=(vmem, smem, vmem),
         scratch_shapes=[
             pltpu.VMEM((PP, 3, BS, BS), BF16),
             pltpu.VMEM((PP, 3, BS, BS), BF16),
@@ -558,7 +564,6 @@
             pltpu.VMEM((8, BS), jnp.int32),
             pltpu.VMEM((NDEV, 8, BS), jnp.int32),
             pltpu.VMEM((8, BS), jnp.int32),
-            pltpu.SMEM((NDEV, 8, BS), jnp.int32),
             pltpu.SMEM((8, BS), jnp.int32),
             pltpu.VMEM((SEC, 2, 2, PH, BS, BS), BF16),
             pltpu.VMEM((SEC, 2, 2, 80, BS), BF16),
@@ -568,28 +573,29 @@
             pltpu.VMEM((3, 2, WCH, BS, BS), BF16),
             pltpu.VMEM((2, WCH, BS, BS), BF16),
             pltpu.VMEM((2, WCH, BS, BS), BF16),
+            pltpu.VMEM((WCH, PP, PP), BF16),
             pltpu.VMEM((WCH, PP * PP, PP * PP), BF16),
             pltpu.VMEM((GRP, PP, BS, BS), BF16),
             pltpu.VMEM((GRP, PP, BS, BS), BF16),
             pltpu.VMEM((2, PP, BS, BS), F32),
-            pltpu.VMEM((8, BS), F32),
-            pltpu.VMEM((NDEV, 8, BS), F32),
-            dma((NDEV,)),
-            dma((NDEV,)),
-            dma((2, NBLK)),
-            dma((2, NBLK)),
-            dma((2, NBLK)),
-            dma((2, NBLK)),
+            pltpu.VMEM((16, BS), F32),
+            pltpu.VMEM((NDEV, 16, BS), F32),
+            dma,
+            dma,
+            dma,
+            dma,
+            dma((2,)),
+            dma((2,)),
             dma((SEC, 2)),
             dma((SEC, 2)),
             dma((SEC, 2)),
             dma((SEC, 2)),
             dma,
             dma,
-            dma((NDEV,)),
-            dma((NDEV,)),
+            dma,
+            dma,
             dma((8,)),
-            dma((2, PP)),
+            dma((2,)),
         ],
         compiler_params=pltpu.CompilerParams(
             collective_id=0, has_side_effects=True, vmem_limit_bytes=VMEM_LIMIT

time: 85.3 us -> 79.9 us (0.937)
  Pallas kernels: 76.7 us -> 72.8 us
  local copies, waits for them, and re-layouts: 7.7 us -> 6.21 us
    pallas_call x1, Pallas kernels: 76.7 us -> 72.8 us  [sweep(): pl.pallas_call(sweep_kernel, out_shape=(pltpu.VMEM((2, BS, M), BF16), jax...]
    unnamed x9 -> x7, local copies, waits for them, and re-layouts: 6.86 us -> 5.37 us
where the time goes in v4:
time: 79.9 us; the launch traced here: 79.7 us
  Pallas kernels  72.8 us (91%)
  local copies, waits for them, and re-layouts  6.21 us (8%)
    pallas_call x1, Pallas kernels, sweep(): pl.pallas_call(sweep_kernel, out_shape=(pltpu.VMEM((2, BS, M), BF16), jax...  72.8 us
    unnamed x7, local copies, waits for them, and re-layouts  5.37 us

profile of v4, /device:TPU:97, one launch (start us, length us, event | category | flops | bytes accessed | tf_op | source)
XLA Modules:
  0.0 79.7 jit_solution(2298270692030711120)
XLA Ops:
  0.6 1.6 %copy.14 = bf16[1,18,16,16]{3,2,1,0:T(8,128)(2,1)} copy(bf16[1,18,16,16]{1,3,2,0:T(8,128)(2,1)} %param.15) | data formatting | bytes 18432 | tf_op args[5]
  2.3 1.2 %copy.15 = bf16[2,4,18,4,18]{4,3,2,1,0:T(4,128)(2,1)S(1)} copy(bf16[2,4,18,4,18]{2,3,1,4,0:T(4,128)(2,1)} %bitcast.15) | data formatting | bytes 41472
  3.5 0.1 pad.8.clone
  3.6 0.1 reshape.9
  3.7 0.6 pad.9.w2_ref
  4.4 72.8 %sweep.1 = (bf16[2,128,2048]{2,1,0:T(8,128)(2,1)S(1)}, f32[1,2]{1,0:T(1,128)}, bf16[2,18,128,128]{3,2,1,0:T(8,128)(2,1)S(1)}) custom-call(s32[18]{0:T(128)} %charge_ref.1, s32[1,2]{1,0:T(1,128)} %len_ref.1, f32[1,2]{1,0:T(1,128)} %energy_ref.1, s32[1,2]{1,0:T(1,128)} %label_ref.1, bf16[2,128,2048]{2,1,0:T(8,128)(2,1)} %bitcast.12, ...), custom_call_target="tpu_custom_call" | custom-call | tf_op jit(solution)/shard_map/sweep/pallas_call | solution.py:550
  77.2 1.0 %copy.19 = bf16[1,2,18,128,128]{4,3,2,1,0:T(8,128)(2,1)} copy(bf16[1,2,18,128,128]{4,3,2,1,0:T(8,128)(2,1)S(1)} %bitcast.9) | data formatting | bytes 2359296
  78.2 0.0 copy-start
  78.2 1.0 %copy.20 = bf16[1,2,128,2048]{3,2,1,0:T(8,128)(2,1)} copy(bf16[1,2,128,2048]{3,2,1,0:T(8,128)(2,1)S(1)} %bitcast.10) | data formatting | bytes 2097152
  79.2 0.0 copy-done
  79.2 0.5 copy.21
Async XLA Ops:
  78.2 1.0 %copy-start = (f32[1,2]{1,0:T(1,128)S(1)}, f32[1,2]{1,0:T(1,128)}, u32[]{:S(2)}) copy-start(f32[1,2]{1,0:T(1,128)} %get-tuple-element.17) | copy-start | bytes 28

commit v5 on v4

--- a/solution.py
+++ b/solution.py
@@ -81,27 +81,44 @@
             l_ref[pl.ds(v + e, BS, stride=WP), :] = one
 
 
-def build_kron(ops_ref, kron):
-    big = (PP * PP, PP)
-    rep = (
-        lax.div(lax.broadcasted_iota(jnp.int32, big, 0), PP)
-        == lax.broadcasted_iota(jnp.int32, big, 1)
-    ).astype(F32).astype(BF16)
-    wide = (PP, PP * PP)
-    rep_t = (
-        lax.div(lax.broadcasted_iota(jnp.int32, wide, 1), PP)
-        == lax.broadcasted_iota(jnp.int32, wide, 0)
-    ).astype(F32).astype(BF16)
+def iota(shape, dim):
+    return lax.broadcasted_iota(jnp.int32, shape, dim)
+
+
+def ones_where(condition):
+    return jnp.where(condition, 1.0, 0.0).astype(BF16)
+
+
+def first_dims(a, b):
+    return lax.dot_general(a, b, (((0,), (0,)), ((), ())), preferred_element_type=F32)
+
+
+def build_mixer(mpo_ref, mixer_ref):
+    tall = (WCH * PP, BS)
+    row, lane = iota(tall, 0), iota(tall, 1)
+    wanted = lax.rem(row, PH) * WP + lax.div(row, PP)
+    place = (80, WCH)
+    for i in range(2):
+        total = jnp.zeros((80, BS), F32)
+        for t in range(PH):
+            pick = ones_where((lax.rem(lax.div(row, PH), PH) == t) & (lane == wanted))
+            part = first_dims(mpo_ref[i], pick).astype(BF16)
+            put = ones_where(iota(place, 0) == t * WCH + iota(place, 1))
+            total = total + mm(put, part)
+        mixer_ref[i] = total.astype(BF16)
+
+
+def build_kron(ops_ref, lines, kron):
     full = (PP * PP, PP * PP)
-    same = lax.rem(lax.broadcasted_iota(jnp.int32, full, 0), PP) == lax.rem(
-        lax.broadcasted_iota(jnp.int32, full, 1), PP
-    )
+    row, lane = iota(full, 0), iota(full, 1)
+    lines[...] = first_dims(ops_ref[...], ones_where(row == lane))
+    spread = ones_where(lax.div(row, PP) == lax.div(lane, PP))
 
     def one(w):
-        rows = lax.dot_general(
-            rep, ops_ref[w], (((1,), (1,)), ((), ())), preferred_element_type=F32
-        ).astype(BF16)
-        kron[w] = jnp.where(same, mm(rows, rep_t), 0.0).astype(BF16)
+        value = jnp.broadcast_to(lines[pl.ds(w, 1), :], full)
+        here = jnp.where(lax.div(row, PP) == lax.rem(lane, PP), value, 0.0).astype(BF16)
+        same = lax.rem(row, PP) == lax.rem(lane, PP)
+        kron[w] = jnp.where(same, mm(here, spread), 0.0).astype(BF16)
 
     loop(0, WCH, one)
 
@@ -149,7 +166,7 @@
     label_ref,
     theta_ref,
     tens_ref,
-    w2_ref,
+    mpo_ref,
     benv_ref,
     right_ref,
     ops_ref,
@@ -173,6 +190,9 @@
     benv,
     right,
     ops,
+    lines,
+    w2_ref,
+    mpo,
     kron,
     mixed,
     states,
@@ -240,11 +260,11 @@
     loads = [
         pltpu.make_async_copy(benv_ref, benv, local.at[0]),
         pltpu.make_async_copy(tens_ref, tens.at[z], local.at[1]),
-        pltpu.make_async_copy(w2_ref, w2.at[z, 0], local.at[2]),
-        pltpu.make_async_copy(w2_ref, w2.at[z, 1], local.at[3]),
         pltpu.make_async_copy(right_ref, right, local.at[4]),
         pltpu.make_async_copy(ops_ref, ops, local.at[6]),
     ]
+    load_mpo = pltpu.make_async_copy(mpo_ref, mpo, local.at[2])
+    load_mpo.start()
     for copy in loads:
         copy.start()
 
@@ -268,6 +288,10 @@
     for turn in range(2):
         arrived(tiles[turn].at[:, 2], tile_sem.at[turn])
     loop(0, PP, mask)
+    load_mpo.wait()
+    build_mixer(mpo, w2_ref)
+    for k in range(2):
+        w2[z, k] = w2_ref[...]
     for turn in range(2):
         recv1[1 + 2 * blk + order[turn]] = tiles[turn][blk, 2]
     pl.semaphore_wait(barrier, NDEV - 1 + SEC - 1)
@@ -341,7 +365,7 @@
 
     for copy in loads:
         copy.wait()
-    build_kron(ops, kron)
+    build_kron(ops, lines, kron)
 
     def load_left(k, env_ref):
         left[k] = jnp.zeros((BS * WP, BS), F32)
@@ -542,7 +566,7 @@
     env_store.wait()
 
 
-def sweep(charges, lens, energy, labels, theta, tensors, w2, benv, right, ops):
+def sweep(charges, lens, energy, labels, theta, tensors, mpo, benv, right, ops):
     hbm = pl.BlockSpec(memory_space=pltpu.HBM)
     vmem = pl.BlockSpec(memory_space=pltpu.VMEM)
     smem = pl.BlockSpec(memory_space=pltpu.SMEM)
@@ -573,7 +597,10 @@
             pltpu.VMEM((3, 2, WCH, BS, BS), BF16),
             pltpu.VMEM((2, WCH, BS, BS), BF16),
             pltpu.VMEM((2, WCH, BS, BS), BF16),
-            pltpu.VMEM((WCH, PP, PP), BF16),
+            pltpu.VMEM((PP * PP, WCH), BF16),
+            pltpu.VMEM((WCH, PP * PP), F32),
+            pltpu.VMEM((2, 80, BS), BF16),
+            pltpu.VMEM((2, WCH * PP, WCH), BF16),
             pltpu.VMEM((WCH, PP * PP, PP * PP), BF16),
             pltpu.VMEM((GRP, PP, BS, BS), BF16),
             pltpu.VMEM((GRP, PP, BS, BS), BF16),
@@ -601,7 +628,7 @@
             collective_id=0, has_side_effects=True, vmem_limit_bytes=VMEM_LIMIT
         ),
         name="sweep",
-    )(charges, lens, energy, labels, theta, tensors, w2, benv, right, ops)
+    )(charges, lens, energy, labels, theta, tensors, mpo, benv, right, ops)
 
 
 def on_device(
@@ -616,10 +643,8 @@
     block_len,
     channel_charge,
 ):
-    w2 = jnp.transpose(site_mpo[0], (0, 3, 2, 4, 1))
-    w2 = jnp.pad(w2, ((0, 0), (0, 0), (0, 0), (0, 0), (0, WP - WCH)))
-    w2 = w2.reshape(2, PH * WCH, PH * WP)
-    w2 = jnp.pad(w2, ((0, 0), (0, 80 - PH * WCH), (0, BS - PH * WP)))
+    mpo = jnp.transpose(site_mpo[0], (0, 1, 3, 4, 2)).reshape(2, WCH * PP, WCH)
+    ops = jnp.transpose(bond_ops[0], (1, 2, 0)).reshape(PP * PP, WCH)
     lanczos, coef, env_out = sweep(
         channel_charge,
         block_len,
@@ -627,10 +652,10 @@
         sector_charge,
         theta[0],
         site_tensors[0],
-        w2,
+        mpo,
         boundary_env,
         right_env[0],
-        bond_ops[0],
+        ops,
     )
     return env_out[None], lanczos[None], coef
 

time: 79.9 us -> 76.6 us (0.959)
  local copies, waits for them, and re-layouts: 6.21 us -> 2.5 us
    unnamed x7 -> x5, local copies, waits for them, and re-layouts: 5.37 us -> 2.5 us
where the time goes in v5:
time: 76.6 us; the launch traced here: 76.5 us
  Pallas kernels  73.3 us (96%)
  local copies, waits for them, and re-layouts  2.5 us (3%)
    pallas_call x1, Pallas kernels, sweep(): pl.pallas_call(sweep_kernel, out_shape=(pltpu.VMEM((2, BS, M), BF16), jax...  73.3 us
    unnamed x5, local copies, waits for them, and re-layouts  2.5 us

profile of v5, /device:TPU:97, one launch (start us, length us, event | category | flops | bytes accessed | tf_op | source)
XLA Modules:
  0.0 76.5 jit_solution(15477510933446464193)
XLA Ops:
  0.6 73.3 %sweep.1 = (bf16[2,128,2048]{2,1,0:T(8,128)(2,1)S(1)}, f32[1,2]{1,0:T(1,128)}, bf16[2,18,128,128]{3,2,1,0:T(8,128)(2,1)S(1)}) custom-call(s32[18]{0:T(128)} %charge_ref.1, s32[1,2]{1,0:T(1,128)} %len_ref.1, f32[1,2]{1,0:T(1,128)} %energy_ref.1, s32[1,2]{1,0:T(1,128)} %label_ref.1, bf16[2,128,2048]{2,1,0:T(8,128)(2,1)} %bitcast.18, ...), custom_call_target="tpu_custom_call" | custom-call | tf_op jit(solution)/shard_map/sweep/pallas_call | solution.py:574
  74.0 1.0 %copy.16 = bf16[1,2,18,128,128]{4,3,2,1,0:T(8,128)(2,1)} copy(bf16[1,2,18,128,128]{4,3,2,1,0:T(8,128)(2,1)S(1)} %bitcast.15) | data formatting | bytes 2359296
  75.0 0.0 copy-start
  75.0 1.0 %copy.17 = bf16[1,2,128,2048]{3,2,1,0:T(8,128)(2,1)} copy(bf16[1,2,128,2048]{3,2,1,0:T(8,128)(2,1)S(1)} %bitcast.16) | data formatting | bytes 2097152
  76.0 0.0 copy-done
  76.0 0.5 copy.18
Async XLA Ops:
  75.0 1.0 %copy-start = (f32[1,2]{1,0:T(1,128)S(1)}, f32[1,2]{1,0:T(1,128)}, u32[]{:S(2)}) copy-start(f32[1,2]{1,0:T(1,128)} %get-tuple-element.17) | copy-start | bytes 28

commit v6 on v5

--- a/solution.py
+++ b/solution.py
@@ -11,7 +11,7 @@
 WP = 24
 MS = 73
 CH = 128
-GRP = 6
+GRP = 9
 PRE = 0
 PP = 16
 M = 2048

time: 76.6 us -> 76.5 us (level)
  no operation moved by 1% of the time
where the time goes in v6:
time: 76.5 us; the launch traced here: 76.3 us
  Pallas kernels  73.2 us (96%)
  local copies, waits for them, and re-layouts  2.5 us (3%)
    pallas_call x1, Pallas kernels, sweep(): pl.pallas_call(sweep_kernel, out_shape=(pltpu.VMEM((2, BS, M), BF16), jax...  73.2 us
    unnamed x5, local copies, waits for them, and re-layouts  2.5 us

profile of v6, /device:TPU:97, one launch (start us, length us, event | category | flops | bytes accessed | tf_op | source)
XLA Modules:
  0.0 76.3 jit_solution(12707437894084392751)
XLA Ops:
  0.6 73.2 %sweep.1 = (bf16[2,128,2048]{2,1,0:T(8,128)(2,1)S(1)}, f32[1,2]{1,0:T(1,128)}, bf16[2,18,128,128]{3,2,1,0:T(8,128)(2,1)S(1)}) custom-call(s32[18]{0:T(128)} %charge_ref.1, s32[1,2]{1,0:T(1,128)} %len_ref.1, f32[1,2]{1,0:T(1,128)} %energy_ref.1, s32[1,2]{1,0:T(1,128)} %label_ref.1, bf16[2,128,2048]{2,1,0:T(8,128)(2,1)} %bitcast.18, ...), custom_call_target="tpu_custom_call" | custom-call | tf_op jit(solution)/shard_map/sweep/pallas_call | solution.py:574
  73.8 1.0 %copy.16 = bf16[1,2,18,128,128]{4,3,2,1,0:T(8,128)(2,1)} copy(bf16[1,2,18,128,128]{4,3,2,1,0:T(8,128)(2,1)S(1)} %bitcast.15) | data formatting | bytes 2359296
  74.9 0.0 copy-start
  74.9 1.0 %copy.17 = bf16[1,2,128,2048]{3,2,1,0:T(8,128)(2,1)} copy(bf16[1,2,128,2048]{3,2,1,0:T(8,128)(2,1)S(1)} %bitcast.16) | data formatting | bytes 2097152
  75.8 0.0 copy-done
  75.8 0.5 copy.18
Async XLA Ops:
  74.9 1.0 %copy-start = (f32[1,2]{1,0:T(1,128)S(1)}, f32[1,2]{1,0:T(1,128)}, u32[]{:S(2)}) copy-start(f32[1,2]{1,0:T(1,128)} %get-tuple-element.17) | copy-start | bytes 28
